TPU v7x, 256 devices: a whole 4x4x8 slice. The times are simulated.
256 devices in a mesh: grp: 8 (over y, x_hi), row: 32 (over z, x_lo, core).
Axes of the slice: x: 4 (x_hi: 2, x_lo: 2; x = x_hi * 2 + x_lo), y: 4, z: 8, core: 2. Of those that a mesh axis runs over, the one named last changes fastest.
Arguments:
- features: float32 [32768, 256], P(('grp', 'row')), may hold values from -6 to 6
- adjacency_tiles: float32 [128, 8, 6, 256, 256], P('row', 'grp'), may hold values from -0.078125 to 0.078125
- tile_cols: int32 [128, 8, 6], P('row', 'grp'), may hold values from 0 to 15, as said below
- tile_count: int32 [128, 8], P('row', 'grp'), may hold values from 1 to 6, as said below
- weight: float32 [256, 256], replicated, may hold values from -0.375 to 0.375
- layer_bias: float32 [256], replicated, may hold values from -3 to 3
- cotangent: float32 [32768, 256], P('row'), may hold values from -6 to 6
Outputs:
- hidden_out: float32 [32768, 256], P('row')
- grad_features: float32 [32768, 256], P(('grp', 'row'))
- grad_weight: float32 [256, 256], replicated
- grad_bias: float32 [256], replicated
Inputs may be any that keep to these rules, and one draw needn't show every extreme that they name: `tile_cols`: for each block row and column range the 6 slots name distinct column blocks. `tile_count`: in every column range some block row has all 6 slots live.
All inputs are finite; a program needn't handle non-finite values.
Results may differ from a plain program's by a relative error of at most 0.0003.
Values sent between devices are 32-bit elements; how exact they have to be, the bound alone decides.
A program may use at most 128 MiB of HBM per device.

v0:
```python
import jax
import jax.numpy as jnp
from jax import lax
from jax.sharding import PartitionSpec as P


def activate(summed, upstream, weight, layer_bias):
    highest = lax.Precision.HIGHEST
    preact = jnp.dot(summed, weight, precision=highest) + layer_bias
    sigma = jax.nn.sigmoid(preact)
    grad_pre = upstream * sigma * (1.0 + preact * (1.0 - sigma))
    return (preact * sigma, grad_pre)


def on_device(features, adjacency_tiles, tile_cols, tile_count, weight, layer_bias, cotangent):
    highest = lax.Precision.HIGHEST
    block_rows, _, slot_count, tile_size, _ = adjacency_tiles.shape
    panel = lax.all_gather(features, "row", axis=0, tiled=True)
    width = panel.shape[1]
    blocks = panel.shape[0] // tile_size
    slots = lax.broadcasted_iota(jnp.int32, (block_rows, slot_count), 1)
    live = (slots < tile_count).astype(jnp.float32)
    block_ids = lax.broadcasted_iota(jnp.int32, (block_rows, slot_count, blocks), 2)
    picks = (tile_cols[:, 0, :, None] == block_ids).astype(jnp.float32) * live[:, :, None]
    local_tiles = adjacency_tiles[:, 0]
    chosen = jnp.einsum(
        "btc,cjf->btjf", picks, panel.reshape(blocks, tile_size, width), precision=highest
    )
    partial_rows = jnp.einsum("btij,btjf->bif", local_tiles, chosen, precision=highest).reshape(
        block_rows * tile_size, width
    )
    scaling = 1.0 / float(block_rows * tile_size * lax.axis_size("row")) ** 0.5
    summed = lax.psum(partial_rows, "grp")
    layer_out, grad_pre = activate(summed, cotangent, weight, layer_bias)
    weight_term = jnp.dot(summed.T, grad_pre, precision=highest) * scaling
    bias_term = jnp.sum(grad_pre, axis=0) * scaling
    grad_weight, grad_bias = lax.psum((weight_term, bias_term), "row")
    backward = jnp.dot(grad_pre, weight.T, precision=highest)
    spread = jnp.einsum(
        "btij,bif->btjf",
        local_tiles,
        backward.reshape(block_rows, tile_size, width),
        precision=highest,
    )
    grad_panel = jnp.einsum("btc,btjf->cjf", picks, spread, precision=highest).reshape(
        blocks * tile_size, width
    )
    grad_owned = lax.psum_scatter(grad_panel, "row", scatter_dimension=0, tiled=True)
    return (layer_out, grad_owned, grad_weight, grad_bias)


def solution(mesh):
    return jax.shard_map(
        on_device,
        mesh=mesh,
        in_specs=(
            P(("grp", "row"), None),
            P("row", "grp", None, None, None),
            P("row", "grp", None),
            P("row", "grp"),
            P(),
            P(),
            P("row", None),
        ),
        out_specs=(P("row", None), P(("grp", "row"), None), P(), P()),
        check_vma=False,
    )
```

profile of v0, /device:TPU:1, one launch (start us, length us, event | category | flops | bytes accessed | tf_op | source)
XLA Modules:
  0.0 562.6 jit_solution(5792356195475707266)
XLA Ops:
  7.2 0.0 copy-start
  7.2 0.0 all-gather.2.cloned.1.call-start
  7.2 0.0 slice-start
  7.2 0.7 all-gather.2.cloned.1.call-update
  7.9 0.0 all-reduce.3.cloned.1.call-start
  8.0 0.7 fusion.19
  8.7 71.9 %all-gather.2.cloned.1.call-done = f32[4096,256]{1,0:T(8,128)} async-done(((f32[128,256]{1,0:T(8,128)}), f32[4096,256]{1,0:T(8,128)}) %all-gather.2.cloned.1.call-update) | async-done | bytes 4194320 | tf_op jit(solution)/shard_map/all_gather | solution.py:18
  80.6 11.8 %fusion.7 = f32[4,6,256,256]{3,1,2,0:T(8,128)S(1)} fusion(f32[16,256,256,1]{2,1,0,3:T(8,128)} %bitcast.47, f32[4,6]{1,0:T(4,128)S(1)} %fusion.19, s32[4,6]{1,0:T(4,128)} %bitcast.50), kind=kOutput, calls=%fused_computation.7 | convolution fusion | flops 301990656 | bytes 10485952 | tf_op jit(solution)/shard_map/btc,cjf->btjf/dot_general | solution.py:26
  92.4 0.0 slice-done
  92.4 0.0 slice-done.1
  92.4 0.0 copy-start.3
  92.4 0.0 copy-start.4
  92.5 9.5 %fusion.4 = f32[4,256,256,1]{1,2,3,0:T(8,128)} fusion(f32[4,1,6,256,256]{4,3,2,1,0:T(8,128)S(1)} %bitcast.45, f32[4,6,256,256]{3,1,2,0:T(8,128)S(1)} %fusion.7), kind=kOutput, calls=%fused_computation.4 | convolution fusion | flops 4831838208 | bytes 13631488 | tf_op jit(solution)/shard_map/btij,btjf->bif/dot_general | solution.py:29
  102.0 0.0 all-reduce.3.cloned.1.call-update
  102.0 0.3 all-reduce.5.cloned.1.call-start
  102.3 90.1 %all-reduce.3.cloned.1.call-done = f32[1024,256]{1,0:T(8,128)} async-done(((f32[1024,256]{1,0:T(8,128)}), f32[1024,256]{1,0:T(8,128)}) %all-reduce.3.cloned.1.call-update) | async-done | bytes 1048592 | tf_op jit(solution)/shard_map/psum | solution.py:33
  192.3 0.0 copy-done
  192.3 0.0 copy-done.3
  192.3 3.6 fusion.22
  195.9 1.0 fusion.23
  196.9 2.5 convolution_multiply_fusion
  199.5 0.0 all-reduce.5.cloned.1.call-update
  199.5 0.0 reduce-scatter.2.cloned.1.call-start
  199.5 11.8 %fusion.2 = f32[4,256,6,256]{3,1,2,0:T(8,128)} fusion(f32[4,256,256,1]{2,1,3,0:T(8,128)S(1)} %bitcast.48, f32[4,1,6,256,256]{4,3,2,1,0:T(8,128)} %param.8), kind=kOutput, calls=%fused_computation.2 | convolution fusion | flops 4831838208 | bytes 13631488 | tf_op jit(solution)/shard_map/btij,bif->btjf/dot_general | solution.py:39
  211.3 9.4 %copy.17 = f32[4,256,6,256]{1,2,0,3:T(8,128)} copy(f32[4,256,6,256]{3,1,2,0:T(8,128)} %fusion.2) | data formatting | bytes 12582912 | tf_op jit(solution)/shard_map/btij,bif->btjf/dot_general | solution.py:39
  220.8 9.3 %fusion.9 = f32[16,256,256]{2,0,1:T(8,128)S(1)} fusion(f32[4,256,6,256]{1,2,0,3:T(8,128)} %copy.17, f32[4,6]{1,0:T(4,128)S(1)} %fusion.19, s32[4,6]{1,0:T(4,128)S(1)} %bitcast.51), kind=kOutput, calls=%fused_computation.9 | convolution fusion | flops 301990656 | bytes 10485952 | tf_op jit(solution)/shard_map/btc,btjf->cjf/dot_general | solution.py:45
  230.1 4.4 copy.11
  234.4 0.0 reduce-scatter.2.cloned.1.call-update
  234.5 58.9 %psum.23 = f32[256]{0:T(256)} all-reduce(f32[256]{0:T(256)S(1)} %broadcast_multiply_fusion), channel_id=1, replica_groups=mesh['grp'=8,'row'=32] {'row'}, use_global_device_ids=true, to_apply=%region_4.0 | all-reduce | flops 256 | bytes 2048 | tf_op jit(solution)/shard_map/psum | solution.py:37
  293.4 136.3 %all-reduce.5.cloned.1.call-done = f32[256,256]{1,0:T(8,128)} async-done(((f32[256,256]{1,0:T(8,128)}), f32[256,256]{1,0:T(8,128)}) %all-reduce.5.cloned.1.call-update) | async-done | bytes 262160 | tf_op jit(solution)/shard_map/psum | solution.py:37
  429.7 124.8 %reduce-scatter.2.cloned.1.call-done = f32[128,256]{1,0:T(8,128)} async-done(((f32[4096,256]{1,0:T(8,128)}), f32[128,256]{1,0:T(8,128)}) %reduce-scatter.2.cloned.1.call-update) | async-done | bytes 131088 | tf_op jit(solution)/shard_map/reduce_scatter | solution.py:48
  554.4 1.7 copy.25
  (8 shorter events, 0.0 us)
Async XLA Ops:
  7.2 185.1 %copy-start = (f32[256,256]{1,0:T(8,128)S(1)}, f32[256,256]{1,0:T(8,128)}, u32[]{:S(2)}) copy-start(f32[256,256]{1,0:T(8,128)} %param.11) | copy-start | bytes 786436
  7.2 73.4 %all-gather.2.cloned.1.call-start = ((), (), s32[]{:S(2)}) async-start(), calls=%async_computation.1 | async-start | bytes 4325376 | tf_op jit(solution)/shard_map/all_gather | solution.py:18
  7.2 85.2 %slice-start = ((s8[6291456]{0:T(1024)(128)(4,1)}), s8[2097152]{0:T(1024)(128)(4,1)S(1)}, s32[]{:S(2)}) async-start(s8[6291456]{0:T(1024)(128)(4,1)} %bitcast.44), calls=%async_computation.5 | async-start | bytes 4194304
  7.9 184.4 %all-reduce.3.cloned.1.call-start = ((), (), s32[]{:S(2)}) async-start(), calls=%async_computation.2 | async-start | bytes 2097152 | tf_op jit(solution)/shard_map/psum | solution.py:33
  80.6 11.9 %slice-start.1 = ((s8[6291456]{0:T(1024)(128)(4,1)}), s8[4194304]{0:T(1024)(128)(4,1)S(1)}, s32[]{:S(2)}) async-start(s8[6291456]{0:T(1024)(128)(4,1)} %bitcast.44), calls=%async_computation.6 | async-start | bytes 8388608
  92.4 99.9 %copy-start.3 = (f32[1024,256]{1,0:T(8,128)S(1)}, f32[1024,256]{1,0:T(8,128)}, u32[]{:S(2)}) copy-start(f32[1024,256]{1,0:T(8,128)} %param.13) | copy-start | bytes 3145732
  92.4 99.9 %copy-start.4 = (f32[256]{0:T(256)S(1)}, f32[256]{0:T(256)}, u32[]{:S(2)}) copy-start(f32[256]{0:T(256)} %param.12) | copy-start | bytes 3076
  102.0 327.7 %all-reduce.5.cloned.1.call-start = ((), (), s32[]{:S(2)}) async-start(), calls=%async_computation.4 | async-start | bytes 524288 | tf_op jit(solution)/shard_map/psum | solution.py:37
  192.3 4.6 copy-start.1
  199.5 354.9 %reduce-scatter.2.cloned.1.call-start = ((), (), s32[]{:S(2)}) async-start(), calls=%async_computation.3 | async-start | bytes 4325376 | tf_op jit(solution)/shard_map/reduce_scatter | solution.py:48
  211.3 9.4 %copy-start.2 = (s32[4,1,6]{2,1,0:T(1,128)S(1)}, s32[4,1,6]{2,1,0:T(1,128)}, u32[]{:S(2)}) copy-start(s32[4,1,6]{2,1,0:T(1,128)} %param.9) | copy-start | bytes 292
Sparse Core Ops, SparseCore 0:
  9.8 70.6 all-gather.1
  102.1 90.1 all-reduce.2
  199.6 230.0 all-reduce.4
  432.6 121.7 reduce-scatter.1
where the time goes:
time: 566 us; the launch traced here: 563 us
  waiting for transfers between devices  424 us (75%)
  blocking collectives  58.9 us (10%)
  matrix products  49.5 us (9%)
  local copies, waits for them, and re-layouts  15.5 us (3%)
  between operations  13.9 us (2%)
    psum x1, waiting for transfers between devices, on_device(): grad_weight, grad_bias = lax.psum((weight_term, bias_term), 'row')  136 us
    reduce_scatter x1, waiting for transfers between devices, on_device(): lax.psum_scatter(grad_panel, 'row', scatter_dimension=0, tiled=True)  125 us
    psum x1, waiting for transfers between devices, on_device(): summed = lax.psum(partial_rows, 'grp')  90.1 us
    all_gather x1, waiting for transfers between devices, on_device(): panel = lax.all_gather(features, 'row', axis=0, tiled=True)  71.9 us
    psum x1, blocking collectives, on_device(): grad_weight, grad_bias = lax.psum((weight_term, bias_term), 'row')  58.9 us
    dot_general x1, matrix products, on_device(): jnp.einsum('btc,cjf->btjf', picks, panel.reshape(blocks, tile_size, width...  11.8 us
    dot_general x1, matrix products, on_device(): jnp.einsum('btij,bif->btjf', local_tiles, backward.reshape(block_rows, ti...  11.8 us
  transfers between devices with their start and end apart: 4, of which 4 were waited for; matrix products, arithmetic and copies ran while one was open for 6% of the time, Pallas kernels for 0%

commit v1 on v0

v1 whole, which is shorter than its diff:
```python
import functools

import jax
import jax.numpy as jnp
from jax import lax
from jax.experimental import pallas as pl
from jax.experimental.pallas import tpu as pltpu
from jax.sharding import PartitionSpec as P

MESH = pl.DeviceIdType.MESH
F32, BF16 = jnp.float32, jnp.bfloat16
NZ, NY = 8, 4
T = 256
AG_Q = 56
RS_Q = 112
N_MSG = 160


def split(x):
    hi = x.astype(BF16)
    return hi, (x - hi.astype(F32)).astype(BF16)


def dot(a, b, ca=1, cb=0):
    return lax.dot_general(a, b, (((ca,), (cb,)), ((), ())), preferred_element_type=F32)


def dot3(a, b, ca=1, cb=0):
    (ah, al), (bh, bl) = a, b
    return dot(ah, bh, ca, cb) + dot(ah, bl, ca, cb) + dot(al, bh, ca, cb)


def kernel(
    scaling,
    feat, tiles, cols, counts, weight, bias, cot,
    hid_out, gf_out, gw_out, gb_out,
    panel, stage, a_hi, a_lo, x_hi, x_lo, w_hi, w_lo, cot_v,
    part, y1, y2, ysum, arx, agg, hid, gw_acc, gb_acc,
    spread, g_send, g_own, g_recv, rx, le, lq, xq,
    gwp, g1, g2, r3, gwo, inv, msk,
    send_sem, recv_sem, load_sem,
):
    row, grp = lax.axis_index("row"), lax.axis_index("grp")
    z, xl, c = lax.div(row, 4), lax.rem(lax.div(row, 2), 2), lax.rem(row, 2)
    y, xh = lax.div(grp, 2), lax.rem(grp, 2)

    def zz(k):
        return lax.rem(z + (k + NZ), NZ)

    def yy(k):
        return lax.rem(y + (k + NY), NY)

    def dev(z_=None, xl_=None, c_=None, y_=None, xh_=None):
        z_, xl_, c_ = z if z_ is None else z_, xl if xl_ is None else xl_, c if c_ is None else c_
        y_, xh_ = y if y_ is None else y_, xh if xh_ is None else xh_
        return {"grp": y_ * 2 + xh_, "row": z_ * 4 + xl_ * 2 + c_}

    def blk(z_, xl_, c_):
        return z_ * 4 + xl_ * 2 + c_

    def m8(v):
        return pl.multiple_of(v, 8)

    msgs = {}

    def push(key, src, dst, device):
        at = len(msgs)
        copy = pltpu.make_async_remote_copy(
            src_ref=src, dst_ref=dst, send_sem=send_sem.at[at], recv_sem=recv_sem.at[at],
            device_id=device, device_id_type=MESH,
        )
        copy.start()
        msgs[key] = copy

    def take(key):
        msgs[key].wait_recv()

    loads = [pltpu.make_async_copy(tiles.at[b, 0], stage.at[b], load_sem.at[b]) for b in range(4)]
    for load in loads:
        load.start()
    cot_load = pltpu.make_async_copy(cot, cot_v, load_sem.at[4])
    cot_load.start()

    barrier = pltpu.get_barrier_semaphore()
    peers = [dev(z_=zz(k)) for k in range(1, NZ)] + [dev(y_=yy(k)) for k in range(1, NY)]
    peers += [dev(xl_=1 - xl), dev(xh_=1 - xh), dev(xl_=1 - xl, xh_=1 - xh), dev(c_=1 - c)]
    for peer in peers:
        pl.semaphore_signal(barrier, inc=1, device_id=peer, device_id_type=MESH)

    own = blk(z, xl, c)
    panel[own] = feat[...]
    wh, wl = split(weight[...])
    w_hi[...] = wh
    w_lo[...] = wl
    pl.semaphore_wait(barrier, len(peers))

    up, down, across, twin = dev(z_=zz(1)), dev(z_=zz(-1)), dev(xl_=1 - xl), dev(c_=1 - c)
    along = {1: up, -1: down}
    for d in (1, -1):
        push(("E", d, 1), feat, panel.at[own], along[d])
    push(("Q", 0), feat.at[pl.ds(0, AG_Q)], panel.at[own, pl.ds(0, AG_Q)], across)
    push(("P", 0), feat.at[pl.ds(AG_Q, 128 - AG_Q)], panel.at[own, pl.ds(AG_Q, 128 - AG_Q)], across)
    push(("SE", 0), feat, panel.at[own], twin)

    def same(key, at, first, count, device):
        ref = panel.at[at, pl.ds(first, count)]
        push(key, ref, ref, device)

    def prepare_tables():
        @pl.loop(0, 64)
        def _(i):
            b, col = lax.div(i, 16), lax.rem(i, 16)
            slot, live = jnp.int32(0), jnp.float32(0)
            for t in range(6):
                hit = jnp.logical_and(cols[b, 0, t] == col, counts[b, 0] > t)
                slot = jnp.where(hit, b * 6 + t, slot)
                live = jnp.where(hit, jnp.float32(1), live)
            inv[i] = slot
            msk[i] = live

    def prepare(b):
        loads[b].wait()
        for t in range(6):
            hi, lo = split(stage[b, t])
            a_hi[b, :, pl.ds(t * T, T)] = hi
            a_lo[b, :, pl.ds(t * T, T)] = lo

    prepare_tables()
    take(("Q", 0))
    for d in (1, -1):
        same(("Q", d, 1), blk(z, 1 - xl, c), 0, AG_Q, along[d])

    q_half = {1: (0, 32), -1: (32, AG_Q - 32)}
    for k in (1, 2, 3):
        for d in (1, -1):
            at = blk(zz(-d * k), xl, c)
            take(("E", d, k))
            if k < 3:
                same(("E", d, k + 1), at, 0, 128, along[d])
            else:
                same(("E", d, 4), at, 0 if d == 1 else 64, 64, along[d])
            same(("P", d * k), at, AG_Q, 128 - AG_Q, across)
            same(("SE", d * k), at, 0, 128, twin)
        for d in (1, -1):
            at = blk(zz(-d * k), 1 - xl, c)
            take(("Q", d, k))
            if k < 3:
                same(("Q", d, k + 1), at, 0, AG_Q, along[d])
            else:
                same(("Q", d, 4), at, *q_half[d], along[d])
        for o in ((0,) if k == 1 else (k - 1, 1 - k)):
            take(("P", o))
            same(("SQ", o), blk(zz(-o), 1 - xl, c), 0, 128, twin)
        prepare(k - 1)
    at = blk(zz(4), xl, c)
    take(("E", 1, 4))
    take(("E", -1, 4))
    same(("P", 4), at, AG_Q, 128 - AG_Q, across)
    same(("SE", 4), at, 0, 128, twin)
    for o in (3, -3):
        take(("P", o))
        same(("SQ", o), blk(zz(-o), 1 - xl, c), 0, 128, twin)
    take(("Q", 1, 4))
    take(("Q", -1, 4))
    prepare(3)
    take(("P", 4))
    same(("SQ", 4), blk(zz(4), 1 - xl, c), 0, 128, twin)
    for o in (0, 1, -1, 2, -2, 3, -3, 4):
        take(("SE", o))
        take(("SQ", o))

    def forward(b):
        for t in range(6):
            at = cols[b, 0, t]
            live = jnp.where(counts[b, 0] > t, jnp.float32(1), jnp.float32(0))
            hi, lo = split(panel[pl.ds(2 * at, 2)].reshape(T, T) * live)
            x_hi[pl.ds(t * T, T), :] = hi
            x_lo[pl.ds(t * T, T), :] = lo
        part[pl.ds(b * T, T), :] = dot3((a_hi[b], a_lo[b]), (x_hi[...], x_lo[...]))

    ahead, behind, opposite = dev(y_=yy(1)), dev(y_=yy(-1)), dev(xh_=1 - xh)

    def rows(b, k, first, count):
        return pl.ds(m8(b * T + yy(k) * 64 + first), count)

    for b in range(4):
        forward(b)
        push(("Y1", 1, b), part.at[rows(b, 2, 0, 32)], y1.at[b, 0], ahead)
        push(("Y1", -1, b), part.at[rows(b, 2, 32, 32)], y1.at[b, 1], behind)
    for b in range(4):
        take(("Y1", 1, b))
        part[rows(b, 1, 0, 32)] += y1[b, 0]
        push(("Y2", 1, b), part.at[rows(b, 1, 0, 64)], y2.at[b, 0], ahead)
        take(("Y1", -1, b))
        part[rows(b, -1, 32, 32)] += y1[b, 1]
        push(("Y2", -1, b), part.at[rows(b, -1, 0, 64)], y2.at[b, 1], behind)
    for b in range(4):
        take(("Y2", 1, b))
        take(("Y2", -1, b))
        ysum[b] = part[rows(b, 0, 0, 64)] + y2[b, 0] + y2[b, 1]
        push(("X", b), ysum.at[b], arx.at[b], opposite)
    for b in range(4):
        take(("X", b))
        agg[rows(b, 0, 0, 64)] = ysum[b] + arx[b]
        mine = agg.at[rows(b, 0, 0, 64)]
        push(("Y3", 1, b), mine, mine, ahead)
        push(("Y3", -1, b), mine, mine, behind)
    for b in range(4):
        take(("Y3", 1, b))
        ref = agg.at[rows(b, -1, 0, 32)]
        push(("Y4", 1, b), ref, ref, ahead)
        take(("Y3", -1, b))
        ref = agg.at[rows(b, 1, 32, 32)]
        push(("Y4", -1, b), ref, ref, behind)

    cot_load.wait()
    stores = []
    for b in range(4):
        take(("Y4", 1, b))
        take(("Y4", -1, b))
        span = pl.ds(b * T, T)
        summed = agg[span, :]
        w = (w_hi[...], w_lo[...])
        pre = dot3(split(summed), w) + bias[...]
        sigma = jax.nn.sigmoid(pre)
        hid[span, :] = pre * sigma
        store = pltpu.make_async_copy(hid.at[span], hid_out.at[span], load_sem.at[5 + b])
        store.start()
        stores.append(store)
        grad = cot_v[span, :] * sigma * (1.0 + pre * (1.0 - sigma))
        gs = split(grad)
        gw = dot3(split(summed.T), gs)
        gb = jnp.sum(grad, axis=0, keepdims=True)
        gw_acc[...] = gw if b == 0 else gw_acc[...] + gw
        gb_acc[...] = gb if b == 0 else gb_acc[...] + gb
        bh, bl = split(dot3(w, gs, 1, 1))
        for t in range(6):
            tile = pl.ds(t * T, T)
            sp = dot3((bh, bl), (a_hi[b, :, tile], a_lo[b, :, tile]))
            spread[b * 6 + t, 0] = sp[:, :128]
            spread[b * 6 + t, 1] = sp[:, 128:]

    gwp[...] = jnp.zeros_like(gwp)
    for c_ in range(2):
        for xl_ in range(2):
            piece = gw_acc[pl.ds(m8(grp * 32 + (xl_ * 2 + c_) * 8), 8), :]
            gwp[c_, xl_, :, pl.ds(0, 256)] = piece * scaling
            gwp[c_, xl_, pl.ds(0, 1), pl.ds(256, 128)] = gb_acc[:, pl.ds(0, 128)] * scaling
            gwp[c_, xl_, pl.ds(1, 1), pl.ds(256, 128)] = gb_acc[:, pl.ds(128, 128)] * scaling
    push(("G1",), gwp.at[1 - c], g1, twin)

    def gather(col, half):
        total = None
        for b in range(4):
            at = b * 16 + col
            term = spread[inv[at], half] * msk[at]
            total = term if total is None else total + term
        return total

    order = (4, 3, -3, 2, -2, 1, -1, 0)
    slot_of = {o: i for i, o in enumerate(order)}

    def col_of(o, other):
        return zz(o) * 2 + ((1 - xl) if other else xl)

    for o in order:
        for other in (True, False):
            col = col_of(o, other)
            g_send[col] = gather(col, 1 - c)
            push(("S", o, other), g_send.at[col], g_recv.at[col], twin)

    p_rows = pl.ds(RS_Q, T - RS_Q)

    def chip_sum(o):
        for other in (True, False):
            col = col_of(o, other)
            mine = gather(col, c)
            take(("S", o, other))
            g_own[col] = mine + g_recv[col]
            if other:
                push(("RX", o), g_own.at[col, p_rows], rx.at[slot_of[o]], across)

    e_half = {1: pl.ds(0, 128), -1: pl.ds(128, 128)}
    r_half = {1: pl.ds(0, 56), -1: pl.ds(56, 56)}

    def ring(k):
        for d in (1, -1):
            col = col_of(d * k, True)
            span = r_half[d] if k == 4 else pl.ds(0, RS_Q)
            if k < 4:
                take(("RQ", d, k + 1))
                got = r_half[d] if k == 3 else span
                g_own[col, got] += lq[0 if d == 1 else 1, k, got]
            push(("RQ", d, k), g_own.at[col, span], lq.at[0 if d == 1 else 1, k - 1, span], along[d])
        for d in (1, -1):
            col = col_of(d * k, False)
            if k < 4 or d == 1:
                take(("RX", d * k))
                g_own[col, p_rows] += rx[slot_of[d * k]]
            span = e_half[d] if k == 4 else pl.ds(0, T)
            if k < 4:
                take(("RE", d, k + 1))
                got = e_half[d] if k == 3 else span
                g_own[col, got] += le[0 if d == 1 else 1, k, got]
            push(("RE", d, k), g_own.at[col, span], le.at[0 if d == 1 else 1, k - 1, span], along[d])

    chip_sum(4)
    chip_sum(3)
    chip_sum(-3)
    ring(4)
    take(("G1",))
    gwp[c] += g1[...]
    push(("G2",), gwp.at[c, 1 - xl], g2, across)
    chip_sum(2)
    chip_sum(-2)
    ring(3)
    take(("G2",))
    r3[z] = gwp[c, xl] + g2[...]
    for k in range(1, NZ):
        push(("G3", k), r3.at[z], r3.at[z], dev(z_=zz(k)))
    chip_sum(1)
    chip_sum(-1)
    chip_sum(0)
    ring(2)
    for k in range(1, NZ):
        take(("G3", k))
    fin = r3[0]
    for k in range(1, NZ):
        fin = fin + r3[k]
    gb_out[:, pl.ds(0, 128)] = fin[0:1, 256:]
    gb_out[:, pl.ds(128, 128)] = fin[1:2, 256:]
    gwo[y, xh, xl, c] = fin[:, :256]
    for k in range(1, NY):
        ref = gwo.at[y, xh, xl, c]
        push(("G4", k), ref, ref, dev(y_=yy(k)))
    ring(1)
    for k in range(1, NY):
        take(("G4", k))
    for i, (a, b) in enumerate(((0, 1), (1, 0), (1, 1))):
        ref = gwo.at[:, xh, xl, c]
        push(("G5", i), ref, ref, dev(xh_=(1 - xh) if a else xh, xl_=(1 - xl) if b else xl))

    col = col_of(0, True)
    q_rows = pl.ds(0, RS_Q)
    for d in (1, -1):
        take(("RQ", d, 1))
        g_own[col, q_rows] += lq[0 if d == 1 else 1, 0, q_rows]
    push(("XF",), g_own.at[col, q_rows], xq, across)
    for i in range(3):
        take(("G5", i))
    ref = gwo.at[:, :, :, c]
    push(("G6",), ref, ref, twin)
    col = col_of(0, False)
    take(("RX", 0))
    g_own[col, p_rows] += rx[slot_of[0]]
    for d in (1, -1):
        take(("RE", d, 1))
    total = g_own[col] + le[0, 0] + le[1, 0]
    g_own[col] = total
    take(("XF",))
    g_own[col, q_rows] += xq[...]
    gf_out[...] = g_own[col].T
    take(("G6",))
    gw_out[...] = gwo[...].reshape(256, 256)

    for store in stores:
        store.wait()
    for copy in msgs.values():
        copy.wait_send()


def on_device(features, tiles, cols, counts, weight, bias, cot):
    n_rows = cot.shape[0]
    scaling = 1.0 / float(n_rows * 32) ** 0.5
    vmem = pl.BlockSpec(memory_space=pltpu.VMEM)
    smem = pl.BlockSpec(memory_space=pltpu.SMEM)
    hbm = pl.BlockSpec(memory_space=pl.ANY)
    shape = jax.ShapeDtypeStruct
    V = pltpu.VMEM
    scratch = [
        V((32, 128, T), F32),
        V((4, 6, T, T), F32),
        V((4, T, 6 * T), BF16), V((4, T, 6 * T), BF16),
        V((6 * T, T), BF16), V((6 * T, T), BF16),
        V((T, T), BF16), V((T, T), BF16),
        V((1024, T), F32),
        V((1024, T), F32),
        V((4, 2, 32, T), F32), V((4, 2, 64, T), F32),
        V((4, 64, T), F32), V((4, 64, T), F32),
        V((1024, T), F32), V((1024, T), F32),
        V((T, T), F32), V((1, T), F32),
        V((24, 2, T, 128), F32),
        V((16, T, 128), F32), V((16, T, 128), F32), V((16, T, 128), F32),
        V((8, T - RS_Q, 128), F32),
        V((2, 4, T, 128), F32), V((2, 4, RS_Q, 128), F32),
        V((RS_Q, 128), F32),
        V((2, 2, 8, 384), F32), V((2, 8, 384), F32), V((8, 384), F32),
        V((8, 8, 384), F32),
        V((4, 2, 2, 2, 8, T), F32),
        pltpu.SMEM((64,), jnp.int32), pltpu.SMEM((64,), F32),
        pltpu.SemaphoreType.DMA((N_MSG,)), pltpu.SemaphoreType.DMA((N_MSG,)),
        pltpu.SemaphoreType.DMA((16,)),
    ]
    hid, gf, gw, gb = pl.pallas_call(
        functools.partial(kernel, scaling),
        out_shape=(
            shape((1024, T), F32), shape((128, T), F32), shape((T, T), F32), shape((1, T), F32),
        ),
        in_specs=[vmem, hbm, smem, smem, vmem, vmem, hbm],
        out_specs=(hbm, vmem, vmem, vmem),
        scratch_shapes=scratch,
        compiler_params=pltpu.CompilerParams(
            collective_id=0, has_side_effects=True, vmem_limit_bytes=60 << 20,
        ),
        name="graph_layer",
    )(features, tiles, cols, counts, weight, bias.reshape(1, T), cot)
    return hid, gf, gw, gb.reshape(T)


def solution(mesh):
    return jax.shard_map(
        on_device,
        mesh=mesh,
        in_specs=(
            P(("grp", "row"), None),
            P("row", "grp", None, None, None),
            P("row", "grp", None),
            P("row", "grp"),
            P(),
            P(),
            P("row", None),
        ),
        out_specs=(P("row", None), P(("grp", "row"), None), P(), P()),
        check_vma=False,
    )
```

time: 566 us -> 105 us (0.19)
  waiting for transfers between devices: 424 us -> 0 us
  Pallas kernels: 0 us -> 95.7 us
  blocking collectives: 58.9 us -> 0 us
  matrix products: 49.5 us -> 0 us
  between operations: 13.9 us -> 0.64 us
  local copies, waits for them, and re-layouts: 15.5 us -> 8.04 us
    psum x2 -> x0, waiting for transfers between devices: 226 us -> none  [the longest x1 136 us: on_device(): grad_weight, grad_bias = lax.psum((weight_term, bias_term), 'row')]
    reduce_scatter x1 -> x0, waiting for transfers between devices: 125 us -> none  [on_device(): lax.psum_scatter(grad_panel, 'row', scatter_dimension=0, tiled=True)]
    pallas_call x0 -> x1, Pallas kernels: none -> 95.7 us  [on_device(): pl.pallas_call(functools.partial(kernel, scaling), out_shape=(shape((1024...]
    all_gather x1 -> x0, waiting for transfers between devices: 71.9 us -> none  [on_device(): panel = lax.all_gather(features, 'row', axis=0, tiled=True)]
    psum x1 -> x0, blocking collectives: 58.9 us -> none  [on_device(): grad_weight, grad_bias = lax.psum((weight_term, bias_term), 'row')]
    dot_general x7 -> x0, matrix products: 49.5 us -> none  [the longest x1 11.8 us: on_device(): jnp.einsum('btc,cjf->btjf', picks, panel.reshape(blocks, tile_size, width...]
    dot_general x2 -> x0, local copies, waits for them, and re-layouts: 13.8 us -> none  [the longest x1 9.43 us: on_device(): jnp.einsum('btij,bif->btjf', local_tiles, backward.reshape(block_rows, ti...]
    unnamed x15 -> x5, local copies, waits for them, and re-layouts: 1.71 us -> 8.04 us
  transfers between devices with their start and end apart: 4 -> 0, of which waited for: 4 -> 0; matrix products, arithmetic and copies ran while one was open for 6% -> 0% of each run, Pallas kernels for 0% -> 0%
where the time goes in v1:
time: 105 us; the launch traced here: 104 us
  Pallas kernels  95.7 us (91%)
  local copies, waits for them, and re-layouts  8.04 us (8%)
    pallas_call x1, Pallas kernels, on_device(): pl.pallas_call(functools.partial(kernel, scaling), out_shape=(shape((1024...  95.7 us
    unnamed x5, local copies, waits for them, and re-layouts  8.04 us

profile of v1, /device:TPU:1, one launch (start us, length us, event | category | flops | bytes accessed | tf_op | source)
XLA Modules:
  0.0 104.4 jit_solution(12592094737847162975)
XLA Ops:
  0.6 1.3 %copy.11.counts = s32[4,1]{1,0:T(4,128)} copy(s32[4,1]{0,1:T(1,128)} %param.10) | data formatting | bytes 32 | tf_op args[3]
  1.9 95.7 %graph_layer.1 = (f32[1024,256]{1,0:T(8,128)}, f32[128,256]{1,0:T(8,128)}, f32[256,256]{1,0:T(8,128)}, f32[1,256]{1,0:T(1,128)}) custom-call(f32[128,256]{1,0:T(8,128)} %feat.1, f32[4,1,6,256,256]{4,3,2,1,0:T(8,128)} %tiles.1, s32[4,1,6]{2,1,0:T(1,128)} %cols.1, s32[4,1]{1,0:T(4,128)} %copy.11.counts, f32[256,256]{1,0:T(8,128)} %weight.1, f32[1,256]{1,0:T(1,128)} %bitcast.2, ...), custom_call_target="tpu_custom_call" | custom-call | tf_op jit(solution)/shard_map/graph_layer/pallas_call | solution.py:404
  97.6 2.3 %copy.16 = f32[1024,256]{1,0:T(8,128)} copy(f32[1024,256]{1,0:T(8,128)} %get-tuple-element.16) | data formatting | bytes 2097152
  99.9 1.6 %copy.17 = f32[128,256]{1,0:T(8,128)} copy(f32[128,256]{1,0:T(8,128)} %get-tuple-element.17) | data formatting | bytes 262144
  101.5 1.7 %copy.18 = f32[256,256]{1,0:T(8,128)} copy(f32[256,256]{1,0:T(8,128)} %get-tuple-element.18) | data formatting | bytes 524288
  103.1 1.2 %copy.19 = f32[256]{0:T(256)} copy(f32[256]{0:T(256)} %bitcast.3) | data formatting | bytes 2048

commit v2 on v1

v2 whole, which is shorter than its diff:
```python
import functools

import jax
import jax.numpy as jnp
from jax import lax
from jax.experimental import pallas as pl
from jax.experimental.pallas import tpu as pltpu
from jax.sharding import PartitionSpec as P

MESH = pl.DeviceIdType.MESH
F32, BF16 = jnp.float32, jnp.bfloat16
NZ, NY = 8, 4
T = 256
AG_Q = 56
RS_Q = 112
N_MSG = 240


def split(x):
    hi = x.astype(BF16)
    return hi, (x - hi.astype(F32)).astype(BF16)


def dot(a, b, ca=1, cb=0):
    return lax.dot_general(a, b, (((ca,), (cb,)), ((), ())), preferred_element_type=F32)


def dot3(a, b, ca=1, cb=0):
    (ah, al), (bh, bl) = a, b
    return dot(ah, bh, ca, cb) + dot(ah, bl, ca, cb) + dot(al, bh, ca, cb)


def kernel(
    scaling,
    feat, tiles, cols_in, counts_in, weight, bias_in, cot,
    hid_out, gf_out, gw_out, gb_out,
    panel_a, panel_b, stage, a_hi, a_lo, x_hi, x_lo, w_v, w_hi, w_lo, bias, cot_v,
    part, y1, y2, ysum, arx, agg, hid, gw_acc, gb_acc,
    spread, g_send, g_own, g_recv, rx, le, lq, xq,
    gwp, g1, g2, r3, gwo, cols, counts, inv, msk,
    send_sem, recv_sem, load_sem,
):
    row, grp = lax.axis_index("row"), lax.axis_index("grp")
    z, xl, c = lax.div(row, 4), lax.rem(lax.div(row, 2), 2), lax.rem(row, 2)
    y, xh = lax.div(grp, 2), lax.rem(grp, 2)

    def zz(k):
        return lax.rem(z + (k + NZ), NZ)

    def yy(k):
        return lax.rem(y + (k + NY), NY)

    def dev(z_=None, xl_=None, c_=None, y_=None, xh_=None):
        z_, xl_, c_ = z if z_ is None else z_, xl if xl_ is None else xl_, c if c_ is None else c_
        y_, xh_ = y if y_ is None else y_, xh if xh_ is None else xh_
        return {"grp": y_ * 2 + xh_, "row": z_ * 4 + xl_ * 2 + c_}

    def blk(z_, xl_, c_):
        return z_ * 4 + xl_ * 2 + c_

    def m8(v):
        return pl.multiple_of(v, 8)

    panels = (panel_a, panel_b)
    msgs = {}

    def push(key, src, dst, device):
        at = len(msgs)
        copy = pltpu.make_async_remote_copy(
            src_ref=src, dst_ref=dst, send_sem=send_sem.at[at], recv_sem=recv_sem.at[at],
            device_id=device, device_id_type=MESH,
        )
        copy.start()
        msgs[key] = copy

    def take(key):
        msgs[key].wait_recv()

    own = blk(z, xl, c)
    n_loads = [0]

    def load(src, dst):
        copy = pltpu.make_async_copy(src, dst, load_sem.at[n_loads[0]])
        copy.start()
        n_loads[0] += 1
        return copy

    barrier = pltpu.get_barrier_semaphore()
    peers = [dev(z_=zz(k)) for k in range(1, NZ)] + [dev(y_=yy(k)) for k in range(1, NY)]
    peers += [dev(xl_=1 - xl), dev(xh_=1 - xh), dev(xl_=1 - xl, xh_=1 - xh), dev(c_=1 - c)]
    for peer in peers:
        pl.semaphore_signal(barrier, inc=1, device_id=peer, device_id_type=MESH)

    feat_loads = [load(feat.at[:, pl.ds(h * 128, 128)], panels[h].at[own]) for h in range(2)]
    small_loads = [load(cols_in, cols), load(counts_in, counts), load(weight, w_v), load(bias_in, bias)]
    tile_loads = [load(tiles.at[b, 0], stage.at[b]) for b in range(4)]
    cot_load = load(cot, cot_v)
    for copy in feat_loads:
        copy.wait()
    pl.semaphore_wait(barrier, len(peers))

    up, down, across, twin = dev(z_=zz(1)), dev(z_=zz(-1)), dev(xl_=1 - xl), dev(c_=1 - c)
    along = {1: up, -1: down}
    both = (1, -1)
    AG_P = 128 - AG_Q
    ep_half = {1: (AG_Q, 40), -1: (AG_Q + 40, AG_P - 40)}
    eq_half = {1: (0, 32), -1: (32, AG_Q - 32)}

    def same(h, key, at, span, device):
        ref = panels[h].at[at, pl.ds(*span)]
        push((h, *key), ref, ref, device)

    def ag_init(h):
        for d in both:
            same(h, ("EP", d, 1), own, (AG_Q, AG_P), along[d])
        same(h, ("Q", 0), own, (0, AG_Q), across)
        for d in both:
            same(h, ("EQ", d, 1), own, (0, AG_Q), along[d])
        same(h, ("P", 0), own, (AG_Q, AG_P), across)
        same(h, ("SE", 0), own, (0, 128), twin)

    def ag_q0(h):
        take((h, "Q", 0))
        for d in both:
            same(h, ("Q", d, 1), blk(z, 1 - xl, c), (0, AG_Q), along[d])

    def ag_crossed(h, o):
        take((h, "P", o))
        same(h, ("SQ", o), blk(zz(-o), 1 - xl, c), (0, 128), twin)

    def ag_hop(h, k):
        for d in both:
            at = blk(zz(-d * k), xl, c)
            take((h, "EP", d, k))
            same(h, ("EP", d, k + 1), at, (AG_Q, AG_P) if k < 3 else ep_half[d], along[d])
            same(h, ("P", d * k), at, (AG_Q, AG_P), across)
        for d in both:
            at = blk(zz(-d * k), xl, c)
            take((h, "EQ", d, k))
            same(h, ("EQ", d, k + 1), at, (0, AG_Q) if k < 3 else eq_half[d], along[d])
            same(h, ("SE", d * k), at, (0, 128), twin)
        for d in both:
            at = blk(zz(-d * k), 1 - xl, c)
            take((h, "Q", d, k))
            same(h, ("Q", d, k + 1), at, (0, AG_Q) if k < 3 else eq_half[d], along[d])
        for o in ((0,) if k == 1 else (k - 1, 1 - k)):
            ag_crossed(h, o)

    def ag_last(h):
        at = blk(zz(4), xl, c)
        for d in both:
            take((h, "EP", d, 4))
        same(h, ("P", 4), at, (AG_Q, AG_P), across)
        for d in both:
            take((h, "EQ", d, 4))
        same(h, ("SE", 4), at, (0, 128), twin)
        ag_crossed(h, 3)
        ag_crossed(h, -3)
        for d in both:
            take((h, "Q", d, 4))

    def ag_end(h):
        ag_crossed(h, 4)
        for o in (0, 1, -1, 2, -2, 3, -3, 4):
            take((h, "SE", o))
            take((h, "SQ", o))

    def prepare_tables():
        for copy in small_loads:
            copy.wait()
        wh, wl = split(w_v[...])
        w_hi[...] = wh
        w_lo[...] = wl

        @pl.loop(0, 64)
        def _(i):
            b, col = lax.div(i, 16), lax.rem(i, 16)
            slot, live = jnp.int32(0), jnp.float32(0)
            for t in range(6):
                hit = jnp.logical_and(cols[b, 0, t] == col, counts[0, b] > t)
                slot = jnp.where(hit, b * 6 + t, slot)
                live = jnp.where(hit, jnp.float32(1), live)
            inv[i] = slot
            msk[i] = live

    def prepare(b):
        tile_loads[b].wait()
        for t in range(6):
            hi, lo = split(stage[b, t])
            a_hi[b, :, pl.ds(t * T, T)] = hi
            a_lo[b, :, pl.ds(t * T, T)] = lo

    def forward(h, b):
        for t in range(6):
            at = cols[b, 0, t]
            live = jnp.where(counts[0, b] > t, jnp.float32(1), jnp.float32(0))
            hi, lo = split(panels[h][pl.ds(2 * at, 2)].reshape(T, 128) * live)
            x_hi[pl.ds(t * T, T), :] = hi
            x_lo[pl.ds(t * T, T), :] = lo
        part[h, pl.ds(b * T, T), :] = dot3((a_hi[b], a_lo[b]), (x_hi[...], x_lo[...]))

    ahead, behind, opposite = dev(y_=yy(1)), dev(y_=yy(-1)), dev(xh_=1 - xh)

    def rows(b, k, first, count):
        return pl.ds(m8(b * T + yy(k) * 64 + first), count)

    def s1(h, b):
        forward(h, b)
        push((h, "Y1", 1, b), part.at[h, rows(b, 2, 0, 32)], y1.at[h, b, 0], ahead)
        push((h, "Y1", -1, b), part.at[h, rows(b, 2, 32, 32)], y1.at[h, b, 1], behind)

    def s2(h, b):
        take((h, "Y1", 1, b))
        part[h, rows(b, 1, 0, 32)] += y1[h, b, 0]
        push((h, "Y2", 1, b), part.at[h, rows(b, 1, 0, 64)], y2.at[h, b, 0], ahead)
        take((h, "Y1", -1, b))
        part[h, rows(b, -1, 32, 32)] += y1[h, b, 1]
        push((h, "Y2", -1, b), part.at[h, rows(b, -1, 0, 64)], y2.at[h, b, 1], behind)

    def s3(h, b):
        take((h, "Y2", 1, b))
        take((h, "Y2", -1, b))
        ysum[h, b] = part[h, rows(b, 0, 0, 64)] + y2[h, b, 0] + y2[h, b, 1]
        push((h, "X", b), ysum.at[h, b], arx.at[h, b], opposite)

    def s4(h, b):
        take((h, "X", b))
        agg[h, rows(b, 0, 0, 64)] = ysum[h, b] + arx[h, b]
        mine = agg.at[h, rows(b, 0, 0, 64)]
        push((h, "Y3", 1, b), mine, mine, ahead)
        push((h, "Y3", -1, b), mine, mine, behind)

    def s5(h, b):
        take((h, "Y3", 1, b))
        ref = agg.at[h, rows(b, -1, 0, 32)]
        push((h, "Y4", 1, b), ref, ref, ahead)
        take((h, "Y3", -1, b))
        ref = agg.at[h, rows(b, 1, 32, 32)]
        push((h, "Y4", -1, b), ref, ref, behind)

    def s6(h, b):
        take((h, "Y4", 1, b))
        take((h, "Y4", -1, b))

    stores = []

    def dense(b):
        span = pl.ds(b * T, T)
        summed = jnp.concatenate([agg[0, span], agg[1, span]], axis=1)
        w = (w_hi[...], w_lo[...])
        pre = dot3(split(summed), w) + bias[...]
        sigma = jax.nn.sigmoid(pre)
        hid[span, :] = pre * sigma
        stores.append(load(hid.at[span], hid_out.at[span]))
        grad = cot_v[span, :] * sigma * (1.0 + pre * (1.0 - sigma))
        gs = split(grad)
        bh, bl = split(dot3(w, gs, 1, 1))
        for t in range(6):
            tile = pl.ds(t * T, T)
            sp = dot3((bh, bl), (a_hi[b, :, tile], a_lo[b, :, tile]))
            spread[b * 6 + t, 0] = sp[:, :128]
            spread[b * 6 + t, 1] = sp[:, 128:]
        gw = dot3(split(summed.T), gs)
        gb = jnp.sum(grad, axis=0, keepdims=True)
        gw_acc[...] = gw if b == 0 else gw_acc[...] + gw
        gb_acc[...] = gb if b == 0 else gb_acc[...] + gb

    ag_init(0)
    prepare_tables()
    ag_q0(0)
    ag_init(1)
    ag_hop(0, 1)
    prepare(0)
    ag_q0(1)
    ag_hop(0, 2)
    ag_hop(1, 1)
    prepare(1)
    ag_hop(0, 3)
    ag_hop(1, 2)
    prepare(2)
    ag_last(0)
    ag_hop(1, 3)
    prepare(3)
    ag_end(0)
    s1(0, 0)
    s1(0, 1)
    ag_last(1)
    s1(0, 2)
    s1(0, 3)
    s2(0, 0)
    s2(0, 1)
    ag_end(1)
    for b in range(4):
        s1(1, b)
        if b < 2:
            s2(0, b + 2)
        if b >= 2:
            s3(0, 2 * b - 4)
            s3(0, 2 * b - 3)
    for b in range(4):
        s4(0, b)
        s2(1, b)
    for b in range(4):
        s5(0, b)
        s3(1, b)
    for b in range(4):
        s4(1, b)
    for b in range(4):
        s6(0, b)
        s5(1, b)
    cot_load.wait()
    for b in range(4):
        s6(1, b)
        dense(b)

    gwp[...] = jnp.zeros_like(gwp)
    for c_ in range(2):
        for xl_ in range(2):
            piece = gw_acc[pl.ds(m8(grp * 32 + (xl_ * 2 + c_) * 8), 8), :]
            gwp[c_, xl_, :, pl.ds(0, 256)] = piece * scaling
            gwp[c_, xl_, pl.ds(0, 1), pl.ds(256, 128)] = gb_acc[:, pl.ds(0, 128)] * scaling
            gwp[c_, xl_, pl.ds(1, 1), pl.ds(256, 128)] = gb_acc[:, pl.ds(128, 128)] * scaling
    push(("G1",), gwp.at[1 - c], g1, twin)

    def gather(col, half):
        total = None
        for b in range(4):
            at = b * 16 + col
            term = spread[inv[at], half] * msk[at]
            total = term if total is None else total + term
        return total

    slot_of = {o: i for i, o in enumerate((4, 3, -3, 2, -2, 1, -1, 0))}
    lane_of = {1: 0, -1: 1}
    RS_P = T - RS_Q
    p_rows, q_rows = pl.ds(RS_Q, RS_P), pl.ds(0, RS_Q)

    def col_of(o, other):
        return zz(o) * 2 + ((1 - xl) if other else xl)

    def to_twin(o):
        for other in (True, False):
            col = col_of(o, other)
            g_send[col] = gather(col, 1 - c)
            push(("S", o, other), g_send.at[col], g_recv.at[col], twin)

    def chip_sum(o):
        for other in (True, False):
            col = col_of(o, other)
            mine = gather(col, c)
            take(("S", o, other))
            g_own[col] = mine + g_recv[col]
            if other:
                push(("RX", o), g_own.at[col, p_rows], rx.at[slot_of[o]], across)

    q_part = {1: pl.ds(0, 56), -1: pl.ds(56, 56)}
    p_part = {1: pl.ds(RS_Q, 72), -1: pl.ds(RS_Q + 72, 72)}

    def ring_q(k):
        for other, name, land in ((True, "RQ", lq), (False, "REQ", le)):
            for d in both:
                col = col_of(d * k, other)
                if k < 4:
                    take((name, d, k + 1))
                    got = q_part[d] if k == 3 else q_rows
                    g_own[col, got] += land[lane_of[d], k, got]
                span = q_part[d] if k == 4 else q_rows
                push((name, d, k), g_own.at[col, span], land.at[lane_of[d], k - 1, span], along[d])

    def ring_p(k):
        for d in both:
            col = col_of(d * k, False)
            if k < 4 or d == 1:
                take(("RX", d * k))
                g_own[col, p_rows] += rx[slot_of[d * k]]
            if k < 4:
                take(("REP", d, k + 1))
                got = p_part[d] if k == 3 else p_rows
                g_own[col, got] += le[lane_of[d], k, got]
            span = p_part[d] if k == 4 else p_rows
            push(("REP", d, k), g_own.at[col, span], le.at[lane_of[d], k - 1, span], along[d])

    to_twin(4)
    to_twin(3)
    to_twin(-3)
    chip_sum(4)
    ring_q(4)
    to_twin(2)
    to_twin(-2)
    chip_sum(3)
    chip_sum(-3)
    ring_p(4)
    to_twin(1)
    to_twin(-1)
    to_twin(0)
    take(("G1",))
    gwp[c] += g1[...]
    push(("G2",), gwp.at[c, 1 - xl], g2, across)
    ring_q(3)
    chip_sum(2)
    chip_sum(-2)
    ring_p(3)
    take(("G2",))
    r3[z] = gwp[c, xl] + g2[...]
    for k in range(1, NZ):
        push(("G3", k), r3.at[z], r3.at[z], dev(z_=zz(k)))
    ring_q(2)
    chip_sum(1)
    chip_sum(-1)
    chip_sum(0)
    ring_p(2)
    for k in range(1, NZ):
        take(("G3", k))
    fin = r3[0]
    for k in range(1, NZ):
        fin = fin + r3[k]
    gb_out[:, pl.ds(0, 128)] = fin[0:1, 256:]
    gb_out[:, pl.ds(128, 128)] = fin[1:2, 256:]
    gwo[y, xh, xl, c] = fin[:, :256]
    for k in range(1, NY):
        ref = gwo.at[y, xh, xl, c]
        push(("G4", k), ref, ref, dev(y_=yy(k)))
    ring_q(1)
    for k in range(1, NY):
        take(("G4", k))
    for i, (a, b) in enumerate(((0, 1), (1, 0), (1, 1))):
        ref = gwo.at[:, xh, xl, c]
        push(("G5", i), ref, ref, dev(xh_=(1 - xh) if a else xh, xl_=(1 - xl) if b else xl))
    ring_p(1)

    col = col_of(0, True)
    for d in both:
        take(("RQ", d, 1))
    g_own[col, q_rows] += lq[0, 0] + lq[1, 0]
    push(("XF",), g_own.at[col, q_rows], xq, across)
    for i in range(3):
        take(("G5", i))
    ref = gwo.at[:, :, :, c]
    push(("G6",), ref, ref, twin)
    col = col_of(0, False)
    for d in both:
        take(("REQ", d, 1))
    take(("RX", 0))
    for d in both:
        take(("REP", d, 1))
    take(("XF",))
    g_own[col, q_rows] += le[0, 0, q_rows] + le[1, 0, q_rows] + xq[...]
    g_own[col, p_rows] += le[0, 0, p_rows] + le[1, 0, p_rows] + rx[slot_of[0]]
    gf_out[...] = g_own[col].T
    take(("G6",))
    gw_out[...] = gwo[...].reshape(256, 256)

    for store in stores:
        store.wait()
    for copy in msgs.values():
        copy.wait_send()


def deliver(hid, gf, gw, gb, hid_out, gf_out, gw_out, gb_out, hid_v, gf_v, gw_v, gb_v, sem_in, sem_out):
    steps = [(hid.at[pl.ds(i * T, T)], hid_v.at[pl.ds(i * T, T)], hid_out.at[pl.ds(i * T, T)]) for i in range(4)]
    steps += [(gf, gf_v, gf_out), (gw, gw_v, gw_out), (gb, gb_v, gb_out)]
    ins = [pltpu.make_async_copy(a, v, sem_in.at[i]) for i, (a, v, _) in enumerate(steps)]
    outs = [pltpu.make_async_copy(v, o, sem_out.at[i]) for i, (_, v, o) in enumerate(steps)]
    for copy in ins:
        copy.start()
    for first, then in zip(ins, outs):
        first.wait()
        then.start()
    for copy in outs:
        copy.wait()


def on_device(features, tiles, cols, counts, weight, bias, cot):
    n_rows = cot.shape[0]
    scaling = 1.0 / float(n_rows * 32) ** 0.5
    vmem = pl.BlockSpec(memory_space=pltpu.VMEM)
    hbm = pl.BlockSpec(memory_space=pl.ANY)
    shape = jax.ShapeDtypeStruct
    V = pltpu.VMEM
    scratch = [
        V((32, 128, 128), F32), V((32, 128, 128), F32),
        V((4, 6, T, T), F32),
        V((4, T, 6 * T), BF16), V((4, T, 6 * T), BF16),
        V((6 * T, 128), BF16), V((6 * T, 128), BF16),
        V((T, T), F32), V((T, T), BF16), V((T, T), BF16),
        V((1, T), F32),
        V((1024, T), F32),
        V((2, 1024, 128), F32),
        V((2, 4, 2, 32, 128), F32), V((2, 4, 2, 64, 128), F32),
        V((2, 4, 64, 128), F32), V((2, 4, 64, 128), F32),
        V((2, 1024, 128), F32), V((1024, T), F32),
        V((T, T), F32), V((1, T), F32),
        V((24, 2, T, 128), F32),
        V((16, T, 128), F32), V((16, T, 128), F32), V((16, T, 128), F32),
        V((8, T - RS_Q, 128), F32),
        V((2, 4, T, 128), F32), V((2, 4, RS_Q, 128), F32),
        V((RS_Q, 128), F32),
        V((2, 2, 8, 384), F32), V((2, 8, 384), F32), V((8, 384), F32),
        V((8, 8, 384), F32),
        V((4, 2, 2, 2, 8, T), F32),
        pltpu.SMEM((4, 1, 6), jnp.int32), pltpu.SMEM((1, 4), jnp.int32),
        pltpu.SMEM((64,), jnp.int32), pltpu.SMEM((64,), F32),
        pltpu.SemaphoreType.DMA((N_MSG,)), pltpu.SemaphoreType.DMA((N_MSG,)),
        pltpu.SemaphoreType.DMA((24,)),
    ]
    outs = (shape((1024, T), F32), shape((128, T), F32), shape((T, T), F32), shape((1, T), F32))
    results = pl.pallas_call(
        functools.partial(kernel, scaling),
        out_shape=outs,
        in_specs=[hbm] * 7,
        out_specs=(hbm, vmem, vmem, vmem),
        scratch_shapes=scratch,
        compiler_params=pltpu.CompilerParams(
            collective_id=0, has_side_effects=True, vmem_limit_bytes=60 << 20,
        ),
        name="graph_layer",
    )(features, tiles, cols, counts.T, weight, bias.reshape(1, T), cot)
    hid, gf, gw, gb = pl.pallas_call(
        deliver,
        out_shape=outs,
        in_specs=[hbm] * 4,
        out_specs=(hbm,) * 4,
        scratch_shapes=[V(o.shape, F32) for o in outs] + [pltpu.SemaphoreType.DMA((7,))] * 2,
        name="deliver",
    )(*results)
    return hid, gf, gw, gb.reshape(T)


def solution(mesh):
    return jax.shard_map(
        on_device,
        mesh=mesh,
        in_specs=(
            P(("grp", "row"), None),
            P("row", "grp", None, None, None),
            P("row", "grp", None),
            P("row", "grp"),
            P(),
            P(),
            P("row", None),
        ),
        out_specs=(P("row", None), P(("grp", "row"), None), P(), P()),
        check_vma=False,
    )
```

time: 105 us -> 97.2 us (0.926)
  local copies, waits for them, and re-layouts: 8.04 us -> 0 us
    unnamed x5 -> x0, local copies, waits for them, and re-layouts: 8.04 us -> none
    pallas_call x1 -> x2, Pallas kernels: 95.7 us -> 96.3 us  [the longest x1 94.1 us: on_device(): pl.pallas_call(functools.partial(kernel, scaling), out_shape=outs, in_spe...]
where the time goes in v2:
time: 97.2 us; the launch traced here: 97.1 us
  Pallas kernels  96.3 us (99%)
    pallas_call x1, Pallas kernels, on_device(): pl.pallas_call(functools.partial(kernel, scaling), out_shape=outs, in_spe...  94.1 us
    pallas_call x1, Pallas kernels, on_device(): pl.pallas_call(deliver, out_shape=outs, in_specs=[hbm] * 4, out_specs=(hb...  2.17 us

profile of v2, /device:TPU:1, one launch (start us, length us, event | category | flops | bytes accessed | tf_op | source)
XLA Modules:
  0.0 97.1 jit_solution(16922098482440672917)
XLA Ops:
  0.6 94.1 %graph_layer.1 = (f32[1024,256]{1,0:T(8,128)}, f32[128,256]{1,0:T(8,128)}, f32[256,256]{1,0:T(8,128)}, f32[1,256]{1,0:T(1,128)}) custom-call(f32[128,256]{1,0:T(8,128)} %feat.1, f32[4,1,6,256,256]{4,3,2,1,0:T(8,128)} %tiles.1, s32[4,1,6]{2,1,0:T(1,128)} %cols_in.1, s32[1,4]{1,0:T(1,128)} %bitcast.4, f32[256,256]{1,0:T(8,128)} %weight.1, f32[1,256]{1,0:T(1,128)} %bitcast.3, ...), custom_call_target="tpu_custom_call" | custom-call | tf_op jit(solution)/shard_map/graph_layer/pallas_call | solution.py:507
  94.8 2.2 %deliver.1 = (f32[1024,256]{1,0:T(8,128)}, f32[128,256]{1,0:T(8,128)}, f32[256,256]{1,0:T(8,128)}, f32[1,256]{1,0:T(1,128)}) custom-call(f32[1024,256]{1,0:T(8,128)} %get-tuple-element.12.hid, f32[128,256]{1,0:T(8,128)} %get-tuple-element.13.gf, f32[256,256]{1,0:T(8,128)} %get-tuple-element.14.gw, f32[1,256]{1,0:T(1,128)} %get-tuple-element.15.gb), custom_call_target="tpu_custom_call" | custom-call | tf_op jit(solution)/shard_map/deliver/pallas_call | solution.py:518

commit v3 on v2

--- a/solution.py
+++ b/solution.py
@@ -13,7 +13,7 @@
 T = 256
 AG_Q = 56
 RS_Q = 112
-N_MSG = 240
+N_MSG, N_SEND = 119, 48
 
 
 def split(x):
@@ -62,19 +62,21 @@
         return pl.multiple_of(v, 8)
 
     panels = (panel_a, panel_b)
-    msgs = {}
-
-    def push(key, src, dst, device):
-        at = len(msgs)
+    sends, groups = [], {}
+
+    def push(group, src, dst, device):
+        at, slot = groups.setdefault(group, len(groups)), len(sends) % N_SEND
+        if len(sends) >= N_SEND:
+            sends[-N_SEND].wait_send()
         copy = pltpu.make_async_remote_copy(
-            src_ref=src, dst_ref=dst, send_sem=send_sem.at[at], recv_sem=recv_sem.at[at],
+            src_ref=src, dst_ref=dst, send_sem=send_sem.at[slot], recv_sem=recv_sem.at[at],
             device_id=device, device_id_type=MESH,
         )
         copy.start()
-        msgs[key] = copy
-
-    def take(key):
-        msgs[key].wait_recv()
+        sends.append(copy)
+
+    def take(group, ref):
+        pltpu.make_async_copy(ref, ref, recv_sem.at[groups[group]]).wait()
 
     own = blk(z, xl, c)
     n_loads = [0]
@@ -110,60 +112,61 @@
         ref = panels[h].at[at, pl.ds(*span)]
         push((h, *key), ref, ref, device)
 
+    def took(h, key, blocks, count):
+        take((h, *key), panels[h].at[pl.ds(0, blocks), pl.ds(0, count)])
+
     def ag_init(h):
-        for d in both:
-            same(h, ("EP", d, 1), own, (AG_Q, AG_P), along[d])
         same(h, ("Q", 0), own, (0, AG_Q), across)
         for d in both:
-            same(h, ("EQ", d, 1), own, (0, AG_Q), along[d])
+            same(h, ("EP", 1), own, (AG_Q, AG_P), along[d])
+        for d in both:
+            same(h, ("EQ", 1), own, (0, AG_Q), along[d])
         same(h, ("P", 0), own, (AG_Q, AG_P), across)
-        same(h, ("SE", 0), own, (0, 128), twin)
-
-    def ag_q0(h):
-        take((h, "Q", 0))
-        for d in both:
-            same(h, ("Q", d, 1), blk(z, 1 - xl, c), (0, AG_Q), along[d])
+        same(h, ("SS",), own, (0, 128), twin)
 
     def ag_crossed(h, o):
-        take((h, "P", o))
-        same(h, ("SQ", o), blk(zz(-o), 1 - xl, c), (0, 128), twin)
-
-    def ag_hop(h, k):
+        took(h, ("P", o), 1, AG_P)
+        same(h, ("SS",), blk(zz(-o), 1 - xl, c), (0, 128), twin)
+
+    def ag_e(h, k):
+        took(h, ("EP", k), 2, AG_P)
         for d in both:
             at = blk(zz(-d * k), xl, c)
-            take((h, "EP", d, k))
-            same(h, ("EP", d, k + 1), at, (AG_Q, AG_P) if k < 3 else ep_half[d], along[d])
-            same(h, ("P", d * k), at, (AG_Q, AG_P), across)
+            same(h, ("EP", k + 1), at, (AG_Q, AG_P) if k < 3 else ep_half[d], along[d])
+        for d in both:
+            same(h, ("P", d * k), blk(zz(-d * k), xl, c), (AG_Q, AG_P), across)
+        took(h, ("EQ", k), 2, AG_Q)
         for d in both:
             at = blk(zz(-d * k), xl, c)
-            take((h, "EQ", d, k))
-            same(h, ("EQ", d, k + 1), at, (0, AG_Q) if k < 3 else eq_half[d], along[d])
-            same(h, ("SE", d * k), at, (0, 128), twin)
+            same(h, ("EQ", k + 1), at, (0, AG_Q) if k < 3 else eq_half[d], along[d])
+        for d in both:
+            same(h, ("SS",), blk(zz(-d * k), xl, c), (0, 128), twin)
+
+    def ag_q(h, k):
+        took(h, ("Q", k), 1 if k == 0 else 2, AG_Q)
         for d in both:
             at = blk(zz(-d * k), 1 - xl, c)
-            take((h, "Q", d, k))
-            same(h, ("Q", d, k + 1), at, (0, AG_Q) if k < 3 else eq_half[d], along[d])
-        for o in ((0,) if k == 1 else (k - 1, 1 - k)):
+            same(h, ("Q", k + 1), at, (0, AG_Q) if k < 3 else eq_half[d], along[d])
+
+    def ag_step(h, k):
+        if k < 4:
+            ag_e(h, k)
+        else:
+            at = blk(zz(4), xl, c)
+            took(h, ("EP", 4), 1, AG_P)
+            same(h, ("P", 4), at, (AG_Q, AG_P), across)
+            took(h, ("EQ", 4), 1, AG_Q)
+            same(h, ("SS",), at, (0, 128), twin)
+        ag_q(h, k - 1)
+        for o in {1: (), 2: (0,), 3: (1, -1), 4: (2, -2)}[k]:
             ag_crossed(h, o)
 
-    def ag_last(h):
-        at = blk(zz(4), xl, c)
-        for d in both:
-            take((h, "EP", d, 4))
-        same(h, ("P", 4), at, (AG_Q, AG_P), across)
-        for d in both:
-            take((h, "EQ", d, 4))
-        same(h, ("SE", 4), at, (0, 128), twin)
+    def ag_end(h):
+        took(h, ("Q", 4), 1, AG_Q)
         ag_crossed(h, 3)
         ag_crossed(h, -3)
-        for d in both:
-            take((h, "Q", d, 4))
-
-    def ag_end(h):
         ag_crossed(h, 4)
-        for o in (0, 1, -1, 2, -2, 3, -3, 4):
-            take((h, "SE", o))
-            take((h, "SQ", o))
+        took(h, ("SS",), 16, 128)
 
     def prepare_tables():
         for copy in small_loads:
@@ -206,41 +209,37 @@
 
     def s1(h, b):
         forward(h, b)
-        push((h, "Y1", 1, b), part.at[h, rows(b, 2, 0, 32)], y1.at[h, b, 0], ahead)
-        push((h, "Y1", -1, b), part.at[h, rows(b, 2, 32, 32)], y1.at[h, b, 1], behind)
+        push((h, "Y1", b), part.at[h, rows(b, 2, 0, 32)], y1.at[h, b, 0], ahead)
+        push((h, "Y1", b), part.at[h, rows(b, 2, 32, 32)], y1.at[h, b, 1], behind)
 
     def s2(h, b):
-        take((h, "Y1", 1, b))
+        take((h, "Y1", b), y1.at[h, b])
         part[h, rows(b, 1, 0, 32)] += y1[h, b, 0]
-        push((h, "Y2", 1, b), part.at[h, rows(b, 1, 0, 64)], y2.at[h, b, 0], ahead)
-        take((h, "Y1", -1, b))
         part[h, rows(b, -1, 32, 32)] += y1[h, b, 1]
-        push((h, "Y2", -1, b), part.at[h, rows(b, -1, 0, 64)], y2.at[h, b, 1], behind)
+        push((h, "Y2", b), part.at[h, rows(b, 1, 0, 64)], y2.at[h, b, 0], ahead)
+        push((h, "Y2", b), part.at[h, rows(b, -1, 0, 64)], y2.at[h, b, 1], behind)
 
     def s3(h, b):
-        take((h, "Y2", 1, b))
-        take((h, "Y2", -1, b))
+        take((h, "Y2", b), y2.at[h, b])
         ysum[h, b] = part[h, rows(b, 0, 0, 64)] + y2[h, b, 0] + y2[h, b, 1]
         push((h, "X", b), ysum.at[h, b], arx.at[h, b], opposite)
 
     def s4(h, b):
-        take((h, "X", b))
+        take((h, "X", b), arx.at[h, b])
         agg[h, rows(b, 0, 0, 64)] = ysum[h, b] + arx[h, b]
         mine = agg.at[h, rows(b, 0, 0, 64)]
-        push((h, "Y3", 1, b), mine, mine, ahead)
-        push((h, "Y3", -1, b), mine, mine, behind)
+        push((h, "Y3", b), mine, mine, ahead)
+        push((h, "Y3", b), mine, mine, behind)
 
     def s5(h, b):
-        take((h, "Y3", 1, b))
+        take((h, "Y3", b), agg.at[h, pl.ds(0, 128)])
         ref = agg.at[h, rows(b, -1, 0, 32)]
-        push((h, "Y4", 1, b), ref, ref, ahead)
-        take((h, "Y3", -1, b))
+        push((h, "Y4", b), ref, ref, ahead)
         ref = agg.at[h, rows(b, 1, 32, 32)]
-        push((h, "Y4", -1, b), ref, ref, behind)
+        push((h, "Y4", b), ref, ref, behind)
 
     def s6(h, b):
-        take((h, "Y4", 1, b))
-        take((h, "Y4", -1, b))
+        take((h, "Y4", b), agg.at[h, pl.ds(0, 64)])
 
     stores = []
 
@@ -267,51 +266,57 @@
 
     ag_init(0)
     prepare_tables()
-    ag_q0(0)
+    ag_step(0, 1)
     ag_init(1)
-    ag_hop(0, 1)
     prepare(0)
-    ag_q0(1)
-    ag_hop(0, 2)
-    ag_hop(1, 1)
+    ag_step(0, 2)
+    ag_step(1, 1)
     prepare(1)
-    ag_hop(0, 3)
-    ag_hop(1, 2)
+    ag_step(0, 3)
+    ag_step(1, 2)
     prepare(2)
-    ag_last(0)
-    ag_hop(1, 3)
+    ag_step(0, 4)
+    ag_step(1, 3)
     prepare(3)
     ag_end(0)
     s1(0, 0)
     s1(0, 1)
-    ag_last(1)
+    ag_step(1, 4)
     s1(0, 2)
     s1(0, 3)
-    s2(0, 0)
-    s2(0, 1)
+    for b in range(4):
+        s2(0, b)
     ag_end(1)
+    s1(1, 0)
+    s3(0, 0)
+    s3(0, 1)
+    s1(1, 1)
+    s3(0, 2)
+    s3(0, 3)
+    s1(1, 2)
+    s1(1, 3)
+    s2(1, 0)
+    s4(0, 0)
+    s2(1, 1)
+    s4(0, 1)
+    s2(1, 2)
+    s4(0, 2)
+    s2(1, 3)
+    s4(0, 3)
     for b in range(4):
-        s1(1, b)
-        if b < 2:
-            s2(0, b + 2)
-        if b >= 2:
-            s3(0, 2 * b - 4)
-            s3(0, 2 * b - 3)
-    for b in range(4):
-        s4(0, b)
-        s2(1, b)
-    for b in range(4):
+        s3(1, b)
         s5(0, b)
-        s3(1, b)
     for b in range(4):
         s4(1, b)
+    cot_load.wait()
     for b in range(4):
         s6(0, b)
         s5(1, b)
-    cot_load.wait()
-    for b in range(4):
-        s6(1, b)
-        dense(b)
+        if b > 0:
+            s6(1, b - 1)
+            dense(b - 1)
+    s6(1, 3)
+    dense(3)
 
     gwp[...] = jnp.zeros_like(gwp)
     for c_ in range(2):
@@ -320,7 +325,38 @@
             gwp[c_, xl_, :, pl.ds(0, 256)] = piece * scaling
             gwp[c_, xl_, pl.ds(0, 1), pl.ds(256, 128)] = gb_acc[:, pl.ds(0, 128)] * scaling
             gwp[c_, xl_, pl.ds(1, 1), pl.ds(256, 128)] = gb_acc[:, pl.ds(128, 128)] * scaling
-    push(("G1",), gwp.at[1 - c], g1, twin)
+    push("G1", gwp.at[1 - c], g1, twin)
+
+    def g_step(i):
+        if i == 1:
+            take("G1", g1)
+            gwp[c] += g1[...]
+            push("G2", gwp.at[c, 1 - xl], g2, across)
+        elif i == 2:
+            take("G2", g2)
+            r3[z] = gwp[c, xl] + g2[...]
+            for k in range(1, NZ):
+                push("G3", r3.at[z], r3.at[z], dev(z_=zz(k)))
+        elif i == 3:
+            take("G3", r3.at[pl.ds(0, NZ - 1)])
+            fin = r3[0]
+            for k in range(1, NZ):
+                fin = fin + r3[k]
+            gb_out[:, pl.ds(0, 128)] = fin[0:1, 256:]
+            gb_out[:, pl.ds(128, 128)] = fin[1:2, 256:]
+            gwo[y, xh, xl, c] = fin[:, :256]
+            for k in range(1, NY):
+                ref = gwo.at[y, xh, xl, c]
+                push("G4", ref, ref, dev(y_=yy(k)))
+        elif i == 4:
+            take("G4", gwo.at[pl.ds(0, NY - 1), 0, 0, 0])
+            ref = gwo.at[:, xh, xl, c]
+            for a, b in ((0, 1), (1, 0), (1, 1)):
+                push("G5", ref, ref, dev(xh_=(1 - xh) if a else xh, xl_=(1 - xl) if b else xl))
+        elif i == 5:
+            take("G5", gwo.at[pl.ds(0, 3), :, :, 0])
+            ref = gwo.at[:, :, :, c]
+            push("G6", ref, ref, twin)
 
     def gather(col, half):
         total = None
@@ -338,18 +374,20 @@
     def col_of(o, other):
         return zz(o) * 2 + ((1 - xl) if other else xl)
 
+    def pair_of(o):
+        return pl.ds(pl.multiple_of(zz(o) * 2, 2), 2)
+
     def to_twin(o):
         for other in (True, False):
             col = col_of(o, other)
             g_send[col] = gather(col, 1 - c)
-            push(("S", o, other), g_send.at[col], g_recv.at[col], twin)
+        push(("S", o), g_send.at[pair_of(o)], g_recv.at[pair_of(o)], twin)
 
     def chip_sum(o):
+        take(("S", o), g_recv.at[pair_of(o)])
         for other in (True, False):
             col = col_of(o, other)
-            mine = gather(col, c)
-            take(("S", o, other))
-            g_own[col] = mine + g_recv[col]
+            g_own[col] = gather(col, c) + g_recv[col]
             if other:
                 push(("RX", o), g_own.at[col, p_rows], rx.at[slot_of[o]], across)
 
@@ -358,101 +396,78 @@
 
     def ring_q(k):
         for other, name, land in ((True, "RQ", lq), (False, "REQ", le)):
+            if k < 4:
+                take((name, k + 1), land.at[0, 0, q_rows] if k == 3 else land.at[:, 0, q_rows])
             for d in both:
                 col = col_of(d * k, other)
                 if k < 4:
-                    take((name, d, k + 1))
                     got = q_part[d] if k == 3 else q_rows
                     g_own[col, got] += land[lane_of[d], k, got]
                 span = q_part[d] if k == 4 else q_rows
-                push((name, d, k), g_own.at[col, span], land.at[lane_of[d], k - 1, span], along[d])
+                push((name, k), g_own.at[col, span], land.at[lane_of[d], k - 1, span], along[d])
 
     def ring_p(k):
+        for o in ((4,) if k == 4 else (k, -k)):
+            take(("RX", o), rx.at[slot_of[o]])
+            g_own[col_of(o, False), p_rows] += rx[slot_of[o]]
+        if k < 4:
+            take(("REP", k + 1), le.at[0, 0, p_rows] if k == 3 else le.at[:, 0, p_rows])
         for d in both:
             col = col_of(d * k, False)
-            if k < 4 or d == 1:
-                take(("RX", d * k))
-                g_own[col, p_rows] += rx[slot_of[d * k]]
             if k < 4:
-                take(("REP", d, k + 1))
                 got = p_part[d] if k == 3 else p_rows
                 g_own[col, got] += le[lane_of[d], k, got]
             span = p_part[d] if k == 4 else p_rows
-            push(("REP", d, k), g_own.at[col, span], le.at[lane_of[d], k - 1, span], along[d])
+            push(("REP", k), g_own.at[col, span], le.at[lane_of[d], k - 1, span], along[d])
 
     to_twin(4)
     to_twin(3)
     to_twin(-3)
     chip_sum(4)
     ring_q(4)
+    chip_sum(3)
+    chip_sum(-3)
+    g_step(1)
     to_twin(2)
     to_twin(-2)
-    chip_sum(3)
-    chip_sum(-3)
-    ring_p(4)
     to_twin(1)
     to_twin(-1)
     to_twin(0)
-    take(("G1",))
-    gwp[c] += g1[...]
-    push(("G2",), gwp.at[c, 1 - xl], g2, across)
-    ring_q(3)
     chip_sum(2)
     chip_sum(-2)
-    ring_p(3)
-    take(("G2",))
-    r3[z] = gwp[c, xl] + g2[...]
-    for k in range(1, NZ):
-        push(("G3", k), r3.at[z], r3.at[z], dev(z_=zz(k)))
-    ring_q(2)
+    ring_q(3)
+    ring_p(4)
     chip_sum(1)
     chip_sum(-1)
     chip_sum(0)
+    g_step(2)
+    ring_q(2)
+    ring_p(3)
+    ring_q(1)
     ring_p(2)
-    for k in range(1, NZ):
-        take(("G3", k))
-    fin = r3[0]
-    for k in range(1, NZ):
-        fin = fin + r3[k]
-    gb_out[:, pl.ds(0, 128)] = fin[0:1, 256:]
-    gb_out[:, pl.ds(128, 128)] = fin[1:2, 256:]
-    gwo[y, xh, xl, c] = fin[:, :256]
-    for k in range(1, NY):
-        ref = gwo.at[y, xh, xl, c]
-        push(("G4", k), ref, ref, dev(y_=yy(k)))
-    ring_q(1)
-    for k in range(1, NY):
-        take(("G4", k))
-    for i, (a, b) in enumerate(((0, 1), (1, 0), (1, 1))):
-        ref = gwo.at[:, xh, xl, c]
-        push(("G5", i), ref, ref, dev(xh_=(1 - xh) if a else xh, xl_=(1 - xl) if b else xl))
+    g_step(3)
+
+    far, near = col_of(0, True), col_of(0, False)
+    take(("RQ", 1), lq.at[:, 0])
+    g_own[far, q_rows] += lq[0, 0] + lq[1, 0]
+    push("XF", g_own.at[far, q_rows], xq, across)
     ring_p(1)
-
-    col = col_of(0, True)
-    for d in both:
-        take(("RQ", d, 1))
-    g_own[col, q_rows] += lq[0, 0] + lq[1, 0]
-    push(("XF",), g_own.at[col, q_rows], xq, across)
-    for i in range(3):
-        take(("G5", i))
-    ref = gwo.at[:, :, :, c]
-    push(("G6",), ref, ref, twin)
-    col = col_of(0, False)
-    for d in both:
-        take(("REQ", d, 1))
-    take(("RX", 0))
-    for d in both:
-        take(("REP", d, 1))
-    take(("XF",))
-    g_own[col, q_rows] += le[0, 0, q_rows] + le[1, 0, q_rows] + xq[...]
-    g_own[col, p_rows] += le[0, 0, p_rows] + le[1, 0, p_rows] + rx[slot_of[0]]
-    gf_out[...] = g_own[col].T
-    take(("G6",))
+    g_step(4)
+    take(("RX", 0), rx.at[slot_of[0]])
+    take(("REQ", 1), le.at[:, 0, q_rows])
+    take("XF", xq)
+    g_own[near, q_rows] += le[0, 0, q_rows] + le[1, 0, q_rows] + xq[...]
+    g_step(5)
+    take(("REP", 1), le.at[:, 0, p_rows])
+    g_own[near, p_rows] += le[0, 0, p_rows] + le[1, 0, p_rows] + rx[slot_of[0]]
+    gf_out[...] = g_own[near].T
+    take("G6", gwo.at[:, :, :, 0])
     gw_out[...] = gwo[...].reshape(256, 256)
 
+    assert len(groups) == N_MSG and n_loads[0] == 15
     for store in stores:
         store.wait()
-    for copy in msgs.values():
+    for copy in sends[-N_SEND:]:
         copy.wait_send()
 
 
@@ -500,8 +515,8 @@
         V((4, 2, 2, 2, 8, T), F32),
         pltpu.SMEM((4, 1, 6), jnp.int32), pltpu.SMEM((1, 4), jnp.int32),
         pltpu.SMEM((64,), jnp.int32), pltpu.SMEM((64,), F32),
-        pltpu.SemaphoreType.DMA((N_MSG,)), pltpu.SemaphoreType.DMA((N_MSG,)),
-        pltpu.SemaphoreType.DMA((24,)),
+        pltpu.SemaphoreType.DMA((N_SEND,)), pltpu.SemaphoreType.DMA((N_MSG,)),
+        pltpu.SemaphoreType.DMA((15,)),
     ]
     outs = (shape((1024, T), F32), shape((128, T), F32), shape((T, T), F32), shape((1, T), F32))
     results = pl.pallas_call(

time: 97.2 us -> 98 us (level)
  no operation moved by 1% of the time
where the time goes in v3:
time: 98 us; the launch traced here: 97.9 us
  Pallas kernels  97.1 us (99%)
    pallas_call x1, Pallas kernels, on_device(): pl.pallas_call(functools.partial(kernel, scaling), out_shape=outs, in_spe...  95 us
    pallas_call x1, Pallas kernels, on_device(): pl.pallas_call(deliver, out_shape=outs, in_specs=[hbm] * 4, out_specs=(hb...  2.17 us

profile of v3, /device:TPU:1, one launch (start us, length us, event | category | flops | bytes accessed | tf_op | source)
XLA Modules:
  0.0 97.9 jit_solution(9028714828711262274)
XLA Ops:
  0.6 95.0 %graph_layer.1 = (f32[1024,256]{1,0:T(8,128)}, f32[128,256]{1,0:T(8,128)}, f32[256,256]{1,0:T(8,128)}, f32[1,256]{1,0:T(1,128)}) custom-call(f32[128,256]{1,0:T(8,128)} %feat.1, f32[4,1,6,256,256]{4,3,2,1,0:T(8,128)} %tiles.1, s32[4,1,6]{2,1,0:T(1,128)} %cols_in.1, s32[1,4]{1,0:T(1,128)} %bitcast.4, f32[256,256]{1,0:T(8,128)} %weight.1, f32[1,256]{1,0:T(1,128)} %bitcast.3, ...), custom_call_target="tpu_custom_call" | custom-call | tf_op jit(solution)/shard_map/graph_layer/pallas_call | solution.py:522
  95.6 2.2 %deliver.1 = (f32[1024,256]{1,0:T(8,128)}, f32[128,256]{1,0:T(8,128)}, f32[256,256]{1,0:T(8,128)}, f32[1,256]{1,0:T(1,128)}) custom-call(f32[1024,256]{1,0:T(8,128)} %get-tuple-element.12.hid, f32[128,256]{1,0:T(8,128)} %get-tuple-element.13.gf, f32[256,256]{1,0:T(8,128)} %get-tuple-element.14.gw, f32[1,256]{1,0:T(1,128)} %get-tuple-element.15.gb), custom_call_target="tpu_custom_call" | custom-call | tf_op jit(solution)/shard_map/deliver/pallas_call | solution.py:533

commit v4 on v3

--- a/solution.py
+++ b/solution.py
@@ -13,7 +13,7 @@
 T = 256
 AG_Q = 56
 RS_Q = 112
-N_MSG, N_SEND = 119, 48
+N_MSG, N_SEND = 188, 48
 
 
 def split(x):
@@ -88,8 +88,11 @@
         return copy
 
     barrier = pltpu.get_barrier_semaphore()
-    peers = [dev(z_=zz(k)) for k in range(1, NZ)] + [dev(y_=yy(k)) for k in range(1, NY)]
-    peers += [dev(xl_=1 - xl), dev(xh_=1 - xh), dev(xl_=1 - xl, xh_=1 - xh), dev(c_=1 - c)]
+    plane = [
+        dev(y_=yy(i // 4), xh_=(1 - xh) if i // 2 % 2 else xh, xl_=(1 - xl) if i % 2 else xl)
+        for i in range(1, 16)
+    ]
+    peers = [dev(z_=zz(k)) for k in range(1, NZ)] + plane + [dev(c_=1 - c)]
     for peer in peers:
         pl.semaphore_signal(barrier, inc=1, device_id=peer, device_id_type=MESH)
 
@@ -118,9 +121,9 @@
     def ag_init(h):
         same(h, ("Q", 0), own, (0, AG_Q), across)
         for d in both:
-            same(h, ("EP", 1), own, (AG_Q, AG_P), along[d])
+            same(h, ("EP", d, 1), own, (AG_Q, AG_P), along[d])
         for d in both:
-            same(h, ("EQ", 1), own, (0, AG_Q), along[d])
+            same(h, ("EQ", d, 1), own, (0, AG_Q), along[d])
         same(h, ("P", 0), own, (AG_Q, AG_P), across)
         same(h, ("SS",), own, (0, 128), twin)
 
@@ -129,42 +132,46 @@
         same(h, ("SS",), blk(zz(-o), 1 - xl, c), (0, 128), twin)
 
     def ag_e(h, k):
-        took(h, ("EP", k), 2, AG_P)
         for d in both:
             at = blk(zz(-d * k), xl, c)
-            same(h, ("EP", k + 1), at, (AG_Q, AG_P) if k < 3 else ep_half[d], along[d])
-        for d in both:
-            same(h, ("P", d * k), blk(zz(-d * k), xl, c), (AG_Q, AG_P), across)
-        took(h, ("EQ", k), 2, AG_Q)
+            took(h, ("EP", d, k), 1, AG_P)
+            same(h, ("EP", d, k + 1), at, (AG_Q, AG_P) if k < 3 else ep_half[d], along[d])
+            same(h, ("P", d * k), at, (AG_Q, AG_P), across)
         for d in both:
             at = blk(zz(-d * k), xl, c)
-            same(h, ("EQ", k + 1), at, (0, AG_Q) if k < 3 else eq_half[d], along[d])
-        for d in both:
-            same(h, ("SS",), blk(zz(-d * k), xl, c), (0, 128), twin)
+            took(h, ("EQ", d, k), 1, AG_Q)
+            same(h, ("EQ", d, k + 1), at, (0, AG_Q) if k < 3 else eq_half[d], along[d])
+            same(h, ("SS",), at, (0, 128), twin)
 
     def ag_q(h, k):
-        took(h, ("Q", k), 1 if k == 0 else 2, AG_Q)
+        if k == 0:
+            took(h, ("Q", 0), 1, AG_Q)
         for d in both:
             at = blk(zz(-d * k), 1 - xl, c)
-            same(h, ("Q", k + 1), at, (0, AG_Q) if k < 3 else eq_half[d], along[d])
+            if k > 0:
+                took(h, ("Q", d, k), 1, AG_Q)
+            same(h, ("Q", d, k + 1), at, (0, AG_Q) if k < 3 else eq_half[d], along[d])
 
     def ag_step(h, k):
         if k < 4:
             ag_e(h, k)
         else:
             at = blk(zz(4), xl, c)
-            took(h, ("EP", 4), 1, AG_P)
+            for d in both:
+                took(h, ("EP", d, 4), 1, ep_half[d][1])
             same(h, ("P", 4), at, (AG_Q, AG_P), across)
-            took(h, ("EQ", 4), 1, AG_Q)
+            for d in both:
+                took(h, ("EQ", d, 4), 1, eq_half[d][1])
             same(h, ("SS",), at, (0, 128), twin)
         ag_q(h, k - 1)
         for o in {1: (), 2: (0,), 3: (1, -1), 4: (2, -2)}[k]:
             ag_crossed(h, o)
 
     def ag_end(h):
-        took(h, ("Q", 4), 1, AG_Q)
         ag_crossed(h, 3)
         ag_crossed(h, -3)
+        for d in both:
+            took(h, ("Q", d, 4), 1, eq_half[d][1])
         ag_crossed(h, 4)
         took(h, ("SS",), 16, 128)
 
@@ -209,14 +216,15 @@
 
     def s1(h, b):
         forward(h, b)
-        push((h, "Y1", b), part.at[h, rows(b, 2, 0, 32)], y1.at[h, b, 0], ahead)
-        push((h, "Y1", b), part.at[h, rows(b, 2, 32, 32)], y1.at[h, b, 1], behind)
+        push((h, "Y1", 1, b), part.at[h, rows(b, 2, 0, 32)], y1.at[h, b, 0], ahead)
+        push((h, "Y1", -1, b), part.at[h, rows(b, 2, 32, 32)], y1.at[h, b, 1], behind)
 
     def s2(h, b):
-        take((h, "Y1", b), y1.at[h, b])
+        take((h, "Y1", 1, b), y1.at[h, b, 0])
         part[h, rows(b, 1, 0, 32)] += y1[h, b, 0]
+        push((h, "Y2", b), part.at[h, rows(b, 1, 0, 64)], y2.at[h, b, 0], ahead)
+        take((h, "Y1", -1, b), y1.at[h, b, 1])
         part[h, rows(b, -1, 32, 32)] += y1[h, b, 1]
-        push((h, "Y2", b), part.at[h, rows(b, 1, 0, 64)], y2.at[h, b, 0], ahead)
         push((h, "Y2", b), part.at[h, rows(b, -1, 0, 64)], y2.at[h, b, 1], behind)
 
     def s3(h, b):
@@ -228,13 +236,14 @@
         take((h, "X", b), arx.at[h, b])
         agg[h, rows(b, 0, 0, 64)] = ysum[h, b] + arx[h, b]
         mine = agg.at[h, rows(b, 0, 0, 64)]
-        push((h, "Y3", b), mine, mine, ahead)
-        push((h, "Y3", b), mine, mine, behind)
+        push((h, "Y3", 1, b), mine, mine, ahead)
+        push((h, "Y3", -1, b), mine, mine, behind)
 
     def s5(h, b):
-        take((h, "Y3", b), agg.at[h, pl.ds(0, 128)])
+        take((h, "Y3", 1, b), agg.at[h, pl.ds(0, 64)])
         ref = agg.at[h, rows(b, -1, 0, 32)]
         push((h, "Y4", b), ref, ref, ahead)
+        take((h, "Y3", -1, b), agg.at[h, pl.ds(0, 64)])
         ref = agg.at[h, rows(b, 1, 32, 32)]
         push((h, "Y4", b), ref, ref, behind)
 
@@ -284,9 +293,11 @@
     ag_step(1, 4)
     s1(0, 2)
     s1(0, 3)
-    for b in range(4):
-        s2(0, b)
+    s2(0, 0)
+    s2(0, 1)
     ag_end(1)
+    s2(0, 2)
+    s2(0, 3)
     s1(1, 0)
     s3(0, 0)
     s3(0, 1)
@@ -294,29 +305,25 @@
     s3(0, 2)
     s3(0, 3)
     s1(1, 2)
-    s1(1, 3)
     s2(1, 0)
     s4(0, 0)
-    s2(1, 1)
-    s4(0, 1)
-    s2(1, 2)
-    s4(0, 2)
-    s2(1, 3)
-    s4(0, 3)
+    s1(1, 3)
     for b in range(4):
+        if b > 0:
+            s4(0, b)
+            s2(1, b)
+    for b in range(4):
+        s5(0, b)
         s3(1, b)
-        s5(0, b)
     for b in range(4):
         s4(1, b)
-    cot_load.wait()
     for b in range(4):
         s6(0, b)
         s5(1, b)
-        if b > 0:
-            s6(1, b - 1)
-            dense(b - 1)
-    s6(1, 3)
-    dense(3)
+    cot_load.wait()
+    for b in range(4):
+        s6(1, b)
+        dense(b)
 
     gwp[...] = jnp.zeros_like(gwp)
     for c_ in range(2):
@@ -326,6 +333,8 @@
             gwp[c_, xl_, pl.ds(0, 1), pl.ds(256, 128)] = gb_acc[:, pl.ds(0, 128)] * scaling
             gwp[c_, xl_, pl.ds(1, 1), pl.ds(256, 128)] = gb_acc[:, pl.ds(128, 128)] * scaling
     push("G1", gwp.at[1 - c], g1, twin)
+
+    chip = y * 4 + xh * 2 + xl
 
     def g_step(i):
         if i == 1:
@@ -344,19 +353,12 @@
                 fin = fin + r3[k]
             gb_out[:, pl.ds(0, 128)] = fin[0:1, 256:]
             gb_out[:, pl.ds(128, 128)] = fin[1:2, 256:]
-            gwo[y, xh, xl, c] = fin[:, :256]
-            for k in range(1, NY):
-                ref = gwo.at[y, xh, xl, c]
-                push("G4", ref, ref, dev(y_=yy(k)))
+            gwo[chip, c] = fin[:, :256]
+            for peer in plane:
+                push("G4", gwo.at[chip, c], gwo.at[chip, c], peer)
         elif i == 4:
-            take("G4", gwo.at[pl.ds(0, NY - 1), 0, 0, 0])
-            ref = gwo.at[:, xh, xl, c]
-            for a, b in ((0, 1), (1, 0), (1, 1)):
-                push("G5", ref, ref, dev(xh_=(1 - xh) if a else xh, xl_=(1 - xl) if b else xl))
-        elif i == 5:
-            take("G5", gwo.at[pl.ds(0, 3), :, :, 0])
-            ref = gwo.at[:, :, :, c]
-            push("G6", ref, ref, twin)
+            take("G4", gwo.at[pl.ds(0, 15), 0])
+            push("G5", gwo.at[:, c], gwo.at[:, c], twin)
 
     def gather(col, half):
         total = None
@@ -391,78 +393,81 @@
             if other:
                 push(("RX", o), g_own.at[col, p_rows], rx.at[slot_of[o]], across)
 
-    q_part = {1: pl.ds(0, 56), -1: pl.ds(56, 56)}
-    p_part = {1: pl.ds(RS_Q, 72), -1: pl.ds(RS_Q + 72, 72)}
+    pieces = {"RQ": (True, 0, 56, lq), "REQ": (False, 0, 56, le), "REP": (False, RS_Q, 72, le)}
+
+    def ring(name, k):
+        other, first, count, land = pieces[name]
+        turns = [(part, d) for part in range(2) for d in both]
+        if k == 4:
+            turns = [(part, d) for part, d in turns if part == lane_of[d]]
+        if k == 3:
+            turns.sort(key=lambda turn: turn[0] == lane_of[turn[1]])
+        for part, d in turns:
+            span = pl.ds(first + part * count, count)
+            col = col_of(d * k, other)
+            if k < 3 or (k == 3 and part == lane_of[d]):
+                take((name, d, part, k + 1), land.at[lane_of[d], k, span])
+                g_own[col, span] += land[lane_of[d], k, span]
+            push((name, d, part, k), g_own.at[col, span], land.at[lane_of[d], k - 1, span], along[d])
+
+    def ring_end(name):
+        other, first, count, land = pieces[name]
+        for part in range(2):
+            for d in both:
+                take((name, d, part, 1), land.at[lane_of[d], 0, pl.ds(first + part * count, count)])
 
     def ring_q(k):
-        for other, name, land in ((True, "RQ", lq), (False, "REQ", le)):
-            if k < 4:
-                take((name, k + 1), land.at[0, 0, q_rows] if k == 3 else land.at[:, 0, q_rows])
-            for d in both:
-                col = col_of(d * k, other)
-                if k < 4:
-                    got = q_part[d] if k == 3 else q_rows
-                    g_own[col, got] += land[lane_of[d], k, got]
-                span = q_part[d] if k == 4 else q_rows
-                push((name, k), g_own.at[col, span], land.at[lane_of[d], k - 1, span], along[d])
+        ring("RQ", k)
+        ring("REQ", k)
 
     def ring_p(k):
-        for o in ((4,) if k == 4 else (k, -k)):
+        for o in (4,) if k == 4 else (k, -k):
             take(("RX", o), rx.at[slot_of[o]])
             g_own[col_of(o, False), p_rows] += rx[slot_of[o]]
-        if k < 4:
-            take(("REP", k + 1), le.at[0, 0, p_rows] if k == 3 else le.at[:, 0, p_rows])
-        for d in both:
-            col = col_of(d * k, False)
-            if k < 4:
-                got = p_part[d] if k == 3 else p_rows
-                g_own[col, got] += le[lane_of[d], k, got]
-            span = p_part[d] if k == 4 else p_rows
-            push(("REP", k), g_own.at[col, span], le.at[lane_of[d], k - 1, span], along[d])
+        ring("REP", k)
 
     to_twin(4)
     to_twin(3)
     to_twin(-3)
     chip_sum(4)
     ring_q(4)
-    chip_sum(3)
-    chip_sum(-3)
     g_step(1)
     to_twin(2)
     to_twin(-2)
+    chip_sum(3)
+    chip_sum(-3)
     to_twin(1)
     to_twin(-1)
     to_twin(0)
+    ring_p(4)
+    ring_q(3)
+    g_step(2)
     chip_sum(2)
     chip_sum(-2)
-    ring_q(3)
-    ring_p(4)
+    ring_p(3)
     chip_sum(1)
     chip_sum(-1)
     chip_sum(0)
-    g_step(2)
     ring_q(2)
-    ring_p(3)
+    g_step(3)
+    ring_p(2)
     ring_q(1)
-    ring_p(2)
-    g_step(3)
+    ring_p(1)
 
     far, near = col_of(0, True), col_of(0, False)
-    take(("RQ", 1), lq.at[:, 0])
+    ring_end("RQ")
     g_own[far, q_rows] += lq[0, 0] + lq[1, 0]
     push("XF", g_own.at[far, q_rows], xq, across)
-    ring_p(1)
     g_step(4)
+    ring_end("REQ")
     take(("RX", 0), rx.at[slot_of[0]])
-    take(("REQ", 1), le.at[:, 0, q_rows])
+    ring_end("REP")
+    g_own[near, p_rows] += le[0, 0, p_rows] + le[1, 0, p_rows] + rx[slot_of[0]]
+    take("G5", gwo.at[:, 0])
+    gw_out[...] = gwo[...].reshape(256, 256)
     take("XF", xq)
     g_own[near, q_rows] += le[0, 0, q_rows] + le[1, 0, q_rows] + xq[...]
-    g_step(5)
-    take(("REP", 1), le.at[:, 0, p_rows])
-    g_own[near, p_rows] += le[0, 0, p_rows] + le[1, 0, p_rows] + rx[slot_of[0]]
     gf_out[...] = g_own[near].T
-    take("G6", gwo.at[:, :, :, 0])
-    gw_out[...] = gwo[...].reshape(256, 256)
 
     assert len(groups) == N_MSG and n_loads[0] == 15
     for store in stores:
@@ -512,7 +517,7 @@
         V((RS_Q, 128), F32),
         V((2, 2, 8, 384), F32), V((2, 8, 384), F32), V((8, 384), F32),
         V((8, 8, 384), F32),
-        V((4, 2, 2, 2, 8, T), F32),
+        V((16, 2, 8, T), F32),
         pltpu.SMEM((4, 1, 6), jnp.int32), pltpu.SMEM((1, 4), jnp.int32),
         pltpu.SMEM((64,), jnp.int32), pltpu.SMEM((64,), F32),
         pltpu.SemaphoreType.DMA((N_SEND,)), pltpu.SemaphoreType.DMA((N_MSG,)),

time: 98 us -> 91.9 us (0.938)
  Pallas kernels: 97.1 us -> 91 us
    pallas_call x1, Pallas kernels: 95 us -> 88.8 us  [on_device(): pl.pallas_call(functools.partial(kernel, scaling), out_shape=outs, in_spe...]
where the time goes in v4:
time: 91.9 us; the launch traced here: 91.8 us
  Pallas kernels  91 us (99%)
    pallas_call x1, Pallas kernels, on_device(): pl.pallas_call(functools.partial(kernel, scaling), out_shape=outs, in_spe...  88.8 us
    pallas_call x1, Pallas kernels, on_device(): pl.pallas_call(deliver, out_shape=outs, in_specs=[hbm] * 4, out_specs=(hb...  2.17 us

profile of v4, /device:TPU:1, one launch (start us, length us, event | category | flops | bytes accessed | tf_op | source)
XLA Modules:
  0.0 91.8 jit_solution(17551845338753713634)
XLA Ops:
  0.6 88.8 %graph_layer.1 = (f32[1024,256]{1,0:T(8,128)}, f32[128,256]{1,0:T(8,128)}, f32[256,256]{1,0:T(8,128)}, f32[1,256]{1,0:T(1,128)}) custom-call(f32[128,256]{1,0:T(8,128)} %feat.1, f32[4,1,6,256,256]{4,3,2,1,0:T(8,128)} %tiles.1, s32[4,1,6]{2,1,0:T(1,128)} %cols_in.1, s32[1,4]{1,0:T(1,128)} %bitcast.4, f32[256,256]{1,0:T(8,128)} %weight.1, f32[1,256]{1,0:T(1,128)} %bitcast.3, ...), custom_call_target="tpu_custom_call" | custom-call | tf_op jit(solution)/shard_map/graph_layer/pallas_call | solution.py:527
  89.4 2.2 %deliver.1 = (f32[1024,256]{1,0:T(8,128)}, f32[128,256]{1,0:T(8,128)}, f32[256,256]{1,0:T(8,128)}, f32[1,256]{1,0:T(1,128)}) custom-call(f32[1024,256]{1,0:T(8,128)} %get-tuple-element.12.hid, f32[128,256]{1,0:T(8,128)} %get-tuple-element.13.gf, f32[256,256]{1,0:T(8,128)} %get-tuple-element.14.gw, f32[1,256]{1,0:T(1,128)} %get-tuple-element.15.gb), custom_call_target="tpu_custom_call" | custom-call | tf_op jit(solution)/shard_map/deliver/pallas_call | solution.py:538

commit v5 on v4

--- a/solution.py
+++ b/solution.py
@@ -92,7 +92,8 @@
         dev(y_=yy(i // 4), xh_=(1 - xh) if i // 2 % 2 else xh, xl_=(1 - xl) if i % 2 else xl)
         for i in range(1, 16)
     ]
-    peers = [dev(z_=zz(k)) for k in range(1, NZ)] + plane + [dev(c_=1 - c)]
+    peers = [dev(z_=zz(1)), dev(z_=zz(-1)), dev(xl_=1 - xl), dev(c_=1 - c)]
+    peers += [dev(y_=yy(1)), dev(y_=yy(-1)), dev(xh_=1 - xh)]
     for peer in peers:
         pl.semaphore_signal(barrier, inc=1, device_id=peer, device_id_type=MESH)
 
@@ -200,14 +201,17 @@
             a_hi[b, :, pl.ds(t * T, T)] = hi
             a_lo[b, :, pl.ds(t * T, T)] = lo
 
-    def forward(h, b):
+    def forward(b):
         for t in range(6):
             at = cols[b, 0, t]
             live = jnp.where(counts[0, b] > t, jnp.float32(1), jnp.float32(0))
-            hi, lo = split(panels[h][pl.ds(2 * at, 2)].reshape(T, 128) * live)
-            x_hi[pl.ds(t * T, T), :] = hi
-            x_lo[pl.ds(t * T, T), :] = lo
-        part[h, pl.ds(b * T, T), :] = dot3((a_hi[b], a_lo[b]), (x_hi[...], x_lo[...]))
+            for h in range(2):
+                hi, lo = split(panels[h][pl.ds(2 * at, 2)].reshape(T, 128) * live)
+                x_hi[pl.ds(t * T, T), pl.ds(h * 128, 128)] = hi
+                x_lo[pl.ds(t * T, T), pl.ds(h * 128, 128)] = lo
+        total = dot3((a_hi[b], a_lo[b]), (x_hi[...], x_lo[...]))
+        for h in range(2):
+            part[h, pl.ds(b * T, T), :] = total[:, h * 128 : h * 128 + 128]
 
     ahead, behind, opposite = dev(y_=yy(1)), dev(y_=yy(-1)), dev(xh_=1 - xh)
 
@@ -215,7 +219,6 @@
         return pl.ds(m8(b * T + yy(k) * 64 + first), count)
 
     def s1(h, b):
-        forward(h, b)
         push((h, "Y1", 1, b), part.at[h, rows(b, 2, 0, 32)], y1.at[h, b, 0], ahead)
         push((h, "Y1", -1, b), part.at[h, rows(b, 2, 32, 32)], y1.at[h, b, 1], behind)
 
@@ -274,55 +277,36 @@
         gb_acc[...] = gb if b == 0 else gb_acc[...] + gb
 
     ag_init(0)
+    ag_init(1)
     prepare_tables()
-    ag_step(0, 1)
-    ag_init(1)
-    prepare(0)
-    ag_step(0, 2)
-    ag_step(1, 1)
-    prepare(1)
-    ag_step(0, 3)
-    ag_step(1, 2)
-    prepare(2)
-    ag_step(0, 4)
-    ag_step(1, 3)
-    prepare(3)
-    ag_end(0)
-    s1(0, 0)
-    s1(0, 1)
-    ag_step(1, 4)
-    s1(0, 2)
-    s1(0, 3)
-    s2(0, 0)
-    s2(0, 1)
-    ag_end(1)
-    s2(0, 2)
-    s2(0, 3)
-    s1(1, 0)
-    s3(0, 0)
-    s3(0, 1)
-    s1(1, 1)
-    s3(0, 2)
-    s3(0, 3)
-    s1(1, 2)
-    s2(1, 0)
-    s4(0, 0)
-    s1(1, 3)
+    for k in range(1, 5):
+        for h in range(2):
+            ag_step(h, k)
+        prepare(k - 1)
+    for h in range(2):
+        ag_end(h)
     for b in range(4):
-        if b > 0:
-            s4(0, b)
-            s2(1, b)
+        if b == 3:
+            for h in range(2):
+                s2(h, 0)
+        forward(b)
+        for h in range(2):
+            s1(h, b)
+    for stage in (s2, s3, s4):
+        for b in range(1 if stage is s2 else 0, 4):
+            for h in range(2):
+                stage(h, b)
     for b in range(4):
-        s5(0, b)
-        s3(1, b)
-    for b in range(4):
-        s4(1, b)
-    for b in range(4):
-        s6(0, b)
-        s5(1, b)
-    cot_load.wait()
-    for b in range(4):
-        s6(1, b)
+        if b == 3:
+            cot_load.wait()
+            for h in range(2):
+                s6(h, 0)
+            dense(0)
+        for h in range(2):
+            s5(h, b)
+    for b in range(1, 4):
+        for h in range(2):
+            s6(h, b)
         dense(b)
 
     gwp[...] = jnp.zeros_like(gwp)
@@ -501,7 +485,7 @@
         V((32, 128, 128), F32), V((32, 128, 128), F32),
         V((4, 6, T, T), F32),
         V((4, T, 6 * T), BF16), V((4, T, 6 * T), BF16),
-        V((6 * T, 128), BF16), V((6 * T, 128), BF16),
+        V((6 * T, T), BF16), V((6 * T, T), BF16),
         V((T, T), F32), V((T, T), BF16), V((T, T), BF16),
         V((1, T), F32),
         V((1024, T), F32),

time: 91.9 us -> 89.5 us (0.974)
  Pallas kernels: 91 us -> 88.7 us
    pallas_call x1, Pallas kernels: 88.8 us -> 86.6 us  [on_device(): pl.pallas_call(functools.partial(kernel, scaling), out_shape=outs, in_spe...]
where the time goes in v5:
time: 89.5 us; the launch traced here: 89.4 us
  Pallas kernels  88.7 us (99%)
    pallas_call x1, Pallas kernels, on_device(): pl.pallas_call(functools.partial(kernel, scaling), out_shape=outs, in_spe...  86.6 us
    pallas_call x1, Pallas kernels, on_device(): pl.pallas_call(deliver, out_shape=outs, in_specs=[hbm] * 4, out_specs=(hb...  2.17 us

profile of v5, /device:TPU:1, one launch (start us, length us, event | category | flops | bytes accessed | tf_op | source)
XLA Modules:
  0.0 89.4 jit_solution(3644513209440154356)
XLA Ops:
  0.6 86.6 %graph_layer.1 = (f32[1024,256]{1,0:T(8,128)}, f32[128,256]{1,0:T(8,128)}, f32[256,256]{1,0:T(8,128)}, f32[1,256]{1,0:T(1,128)}) custom-call(f32[128,256]{1,0:T(8,128)} %feat.1, f32[4,1,6,256,256]{4,3,2,1,0:T(8,128)} %tiles.1, s32[4,1,6]{2,1,0:T(1,128)} %cols_in.1, s32[1,4]{1,0:T(1,128)} %bitcast.4, f32[256,256]{1,0:T(8,128)} %weight.1, f32[1,256]{1,0:T(1,128)} %bitcast.3, ...), custom_call_target="tpu_custom_call" | custom-call | tf_op jit(solution)/shard_map/graph_layer/pallas_call | solution.py:511
  87.2 2.2 %deliver.1 = (f32[1024,256]{1,0:T(8,128)}, f32[128,256]{1,0:T(8,128)}, f32[256,256]{1,0:T(8,128)}, f32[1,256]{1,0:T(1,128)}) custom-call(f32[1024,256]{1,0:T(8,128)} %get-tuple-element.12.hid, f32[128,256]{1,0:T(8,128)} %get-tuple-element.13.gf, f32[256,256]{1,0:T(8,128)} %get-tuple-element.14.gw, f32[1,256]{1,0:T(1,128)} %get-tuple-element.15.gb), custom_call_target="tpu_custom_call" | custom-call | tf_op jit(solution)/shard_map/deliver/pallas_call | solution.py:522

commit v6 on v5

--- a/solution.py
+++ b/solution.py
@@ -13,7 +13,7 @@
 T = 256
 AG_Q = 56
 RS_Q = 112
-N_MSG, N_SEND = 188, 48
+N_MSG, N_SEND = 189, 36
 
 
 def split(x):
@@ -286,25 +286,15 @@
     for h in range(2):
         ag_end(h)
     for b in range(4):
-        if b == 3:
-            for h in range(2):
-                s2(h, 0)
         forward(b)
         for h in range(2):
             s1(h, b)
-    for stage in (s2, s3, s4):
-        for b in range(1 if stage is s2 else 0, 4):
+    for stage in (s2, s3, s4, s5):
+        for b in range(4):
             for h in range(2):
                 stage(h, b)
+    cot_load.wait()
     for b in range(4):
-        if b == 3:
-            cot_load.wait()
-            for h in range(2):
-                s6(h, 0)
-            dense(0)
-        for h in range(2):
-            s5(h, b)
-    for b in range(1, 4):
         for h in range(2):
             s6(h, b)
         dense(b)
@@ -394,11 +384,10 @@
                 g_own[col, span] += land[lane_of[d], k, span]
             push((name, d, part, k), g_own.at[col, span], land.at[lane_of[d], k - 1, span], along[d])
 
-    def ring_end(name):
+    def ring_end(name, part):
         other, first, count, land = pieces[name]
-        for part in range(2):
-            for d in both:
-                take((name, d, part, 1), land.at[lane_of[d], 0, pl.ds(first + part * count, count)])
+        for d in both:
+            take((name, d, part, 1), land.at[lane_of[d], 0, pl.ds(first + part * count, count)])
 
     def ring_q(k):
         ring("RQ", k)
@@ -439,17 +428,22 @@
     ring_p(1)
 
     far, near = col_of(0, True), col_of(0, False)
-    ring_end("RQ")
-    g_own[far, q_rows] += lq[0, 0] + lq[1, 0]
-    push("XF", g_own.at[far, q_rows], xq, across)
+    for part in range(2):
+        ring_end("RQ", part)
+        span = pl.ds(part * 56, 56)
+        g_own[far, span] += lq[0, 0, span] + lq[1, 0, span]
+        push(("XF", part), g_own.at[far, span], xq.at[span], across)
     g_step(4)
-    ring_end("REQ")
+    for part in range(2):
+        ring_end("REQ", part)
     take(("RX", 0), rx.at[slot_of[0]])
-    ring_end("REP")
+    for part in range(2):
+        ring_end("REP", part)
     g_own[near, p_rows] += le[0, 0, p_rows] + le[1, 0, p_rows] + rx[slot_of[0]]
     take("G5", gwo.at[:, 0])
     gw_out[...] = gwo[...].reshape(256, 256)
-    take("XF", xq)
+    for part in range(2):
+        take(("XF", part), xq.at[pl.ds(part * 56, 56)])
     g_own[near, q_rows] += le[0, 0, q_rows] + le[1, 0, q_rows] + xq[...]
     gf_out[...] = g_own[near].T
 

time: 89.5 us -> 88.2 us (0.985)
  Pallas kernels: 88.7 us -> 87.4 us
    pallas_call x1, Pallas kernels: 86.6 us -> 85.3 us  [on_device(): pl.pallas_call(functools.partial(kernel, scaling), out_shape=outs, in_spe...]
where the time goes in v6:
time: 88.2 us; the launch traced here: 88.1 us
  Pallas kernels  87.4 us (99%)
    pallas_call x1, Pallas kernels, on_device(): pl.pallas_call(functools.partial(kernel, scaling), out_shape=outs, in_spe...  85.3 us
    pallas_call x1, Pallas kernels, on_device(): pl.pallas_call(deliver, out_shape=outs, in_specs=[hbm] * 4, out_specs=(hb...  2.17 us

profile of v6, /device:TPU:1, one launch (start us, length us, event | category | flops | bytes accessed | tf_op | source)
XLA Modules:
  0.0 88.1 jit_solution(11901356782998060439)
XLA Ops:
  0.6 85.3 %graph_layer.1 = (f32[1024,256]{1,0:T(8,128)}, f32[128,256]{1,0:T(8,128)}, f32[256,256]{1,0:T(8,128)}, f32[1,256]{1,0:T(1,128)}) custom-call(f32[128,256]{1,0:T(8,128)} %feat.1, f32[4,1,6,256,256]{4,3,2,1,0:T(8,128)} %tiles.1, s32[4,1,6]{2,1,0:T(1,128)} %cols_in.1, s32[1,4]{1,0:T(1,128)} %bitcast.4, f32[256,256]{1,0:T(8,128)} %weight.1, f32[1,256]{1,0:T(1,128)} %bitcast.3, ...), custom_call_target="tpu_custom_call" | custom-call | tf_op jit(solution)/shard_map/graph_layer/pallas_call | solution.py:505
  85.9 2.2 %deliver.1 = (f32[1024,256]{1,0:T(8,128)}, f32[128,256]{1,0:T(8,128)}, f32[256,256]{1,0:T(8,128)}, f32[1,256]{1,0:T(1,128)}) custom-call(f32[1024,256]{1,0:T(8,128)} %get-tuple-element.12.hid, f32[128,256]{1,0:T(8,128)} %get-tuple-element.13.gf, f32[256,256]{1,0:T(8,128)} %get-tuple-element.14.gw, f32[1,256]{1,0:T(1,128)} %get-tuple-element.15.gb), custom_call_target="tpu_custom_call" | custom-call | tf_op jit(solution)/shard_map/deliver/pallas_call | solution.py:516

commit v7 on v6

--- a/solution.py
+++ b/solution.py
@@ -11,7 +11,7 @@
 F32, BF16 = jnp.float32, jnp.bfloat16
 NZ, NY = 8, 4
 T = 256
-AG_Q = 56
+AG_Q = 48
 RS_Q = 112
 N_MSG, N_SEND = 189, 36
 

time: 88.2 us -> 88.4 us (level)
  no operation moved by 1% of the time
where the time goes in v7:
time: 88.4 us; the launch traced here: 88.3 us
  Pallas kernels  87.7 us (99%)
    pallas_call x1, Pallas kernels, on_device(): pl.pallas_call(functools.partial(kernel, scaling), out_shape=outs, in_spe...  85.5 us
    pallas_call x1, Pallas kernels, on_device(): pl.pallas_call(deliver, out_shape=outs, in_specs=[hbm] * 4, out_specs=(hb...  2.17 us

profile of v7, /device:TPU:1, one launch (start us, length us, event | category | flops | bytes accessed | tf_op | source)
XLA Modules:
  0.0 88.3 jit_solution(9088118813407468146)
XLA Ops:
  0.6 85.5 %graph_layer.1 = (f32[1024,256]{1,0:T(8,128)}, f32[128,256]{1,0:T(8,128)}, f32[256,256]{1,0:T(8,128)}, f32[1,256]{1,0:T(1,128)}) custom-call(f32[128,256]{1,0:T(8,128)} %feat.1, f32[4,1,6,256,256]{4,3,2,1,0:T(8,128)} %tiles.1, s32[4,1,6]{2,1,0:T(1,128)} %cols_in.1, s32[1,4]{1,0:T(1,128)} %bitcast.4, f32[256,256]{1,0:T(8,128)} %weight.1, f32[1,256]{1,0:T(1,128)} %bitcast.3, ...), custom_call_target="tpu_custom_call" | custom-call | tf_op jit(solution)/shard_map/graph_layer/pallas_call | solution.py:505
  86.1 2.2 %deliver.1 = (f32[1024,256]{1,0:T(8,128)}, f32[128,256]{1,0:T(8,128)}, f32[256,256]{1,0:T(8,128)}, f32[1,256]{1,0:T(1,128)}) custom-call(f32[1024,256]{1,0:T(8,128)} %get-tuple-element.12.hid, f32[128,256]{1,0:T(8,128)} %get-tuple-element.13.gf, f32[256,256]{1,0:T(8,128)} %get-tuple-element.14.gw, f32[1,256]{1,0:T(1,128)} %get-tuple-element.15.gb), custom_call_target="tpu_custom_call" | custom-call | tf_op jit(solution)/shard_map/deliver/pallas_call | solution.py:516
